TPU v7x, 128 devices: a whole 4x4x4 slice. The times are simulated.
128 devices in a mesh: ang: 16 (over z_hi, x, core), hgt: 8 (over z_lo, y).
Axes of the slice: x: 4, y: 4, z: 4 (z_hi: 2, z_lo: 2; z = z_hi * 2 + z_lo), core: 2. Of those that a mesh axis runs over, the one named last changes fastest.
Arguments:
- loads: float32 [4, 3, 512, 64, 128], P(None, None, 'ang', 'hgt'), may hold values from -6 to 6
- material: int32 [512, 64, 128], P('ang', 'hgt'), may hold values from 0 to 7
- support: int32 [512, 64, 128], P('ang', 'hgt'), may hold values 0 or 1
- modulus: float32 [8], replicated, may hold values from 0.5 to 5
- positions: int32 [4], replicated, may hold values from 0 to 511
Outputs:
- solution_field: float32 [4, 3, 512, 64, 128], P(None, None, 'ang', 'hgt')
- residual: float32 [4, 3, 512, 64, 128], P(None, None, 'ang', 'hgt')
All inputs are finite; a program needn't handle non-finite values. No bound on the sum of `support` on one device may be relied on, other than what follows from the above.
Results may differ from a plain program's by a relative error of at most 0.0003.
Values sent between devices are 32-bit elements; how exact they have to be, the bound alone decides.
A program may use at most 64 MiB of HBM per device.

v0:
```python
import jax
import jax.numpy as jnp
from jax import lax
from jax.sharding import PartitionSpec as P

ITERS = 3
CSWEEPS = 4


SIGMA = 6.5
SPRING = 20.0
OMEGA = 0.8
LOAD = 3.0


def padded_2(block, sides, width, periodic):
    for axis, dim in sides:
        count = lax.axis_size(axis)
        forward = [(i, i + 1) for i in range(count - 1)]
        if periodic:
            forward.append((count - 1, 0))
        backward = [(target, source) for source, target in forward]
        low = lax.ppermute(
            lax.slice_in_dim(block, block.shape[dim] - width, None, axis=dim), axis, forward
        )
        high = lax.ppermute(lax.slice_in_dim(block, 0, width, axis=dim), axis, backward)
        block = jnp.concatenate([low, block, high], axis=dim)
    return block


def zero_pair(v, axis):
    widths = [(0, 0)] * v.ndim
    widths[axis] = (1, 1)
    padded = jnp.pad(v, widths)
    size = v.shape[axis]
    return lax.slice_in_dim(padded, 2, size + 2, axis=axis) + lax.slice_in_dim(
        padded, 0, size, axis=axis
    )


def fine_apply(u, weight, spring):
    v = weight * u
    beside_all = padded_2(v, (("ang", 2),), 1, True)
    above = padded_2(v, (("hgt", 3),), 1, False)
    beside = beside_all[:, :, 2:] + beside_all[:, :, :-2] + above[:, :, :, 2:] + above[:, :, :, :-2]
    beside = beside + zero_pair(v, 4)
    return weight * (SIGMA * v - beside) + SPRING * spring * u


def split_apply(u, weight, spring):
    v = weight * u
    beside_all = padded_2(v, (("ang", 2),), 1, True)
    above = padded_2(v, (("hgt", 3),), 1, False)
    beside = beside_all[:, :, 2:] + beside_all[:, :, :-2] + above[:, :, :, 2:] + above[:, :, :, :-2]
    beside = beside + zero_pair(v, 4)
    return weight * (SIGMA * v - beside) + SPRING * spring * u


def coarsen(field):
    a, h, r = field.shape
    return field.reshape(a // 2, 2, h // 2, 2, r).mean(axis=(1, 3))


def restrict(r):
    c, k, a, h, n = r.shape
    return r.reshape(c, k, a // 2, 2, h // 2, 2, n).sum(axis=(3, 5)) * 0.5


def prolong(e):
    return jnp.repeat(jnp.repeat(e, 2, axis=2), 2, axis=3) * 0.5


def body(loads, material, support, modulus, positions):
    cases, comps, a_dev, h_dev, radial = loads.shape
    levels = lax.iota(jnp.int32, modulus.shape[0])
    stiff = jnp.sum(
        jnp.where(material[None] == levels[:, None, None, None], modulus[:, None, None, None], 0.0),
        axis=0,
    )
    weight = jnp.sqrt(stiff)
    spring = support.astype(jnp.float32)
    diag = SIGMA * weight * weight + SPRING * spring
    wide_c = coarsen(weight)
    spring_c = coarsen(spring)
    diag_c = SIGMA * wide_c * wide_c + SPRING * spring_c
    total_angles = a_dev * lax.axis_size("ang")
    angles = lax.axis_index("ang") * a_dev + lax.iota(jnp.int32, a_dev)
    apart = jnp.abs(angles[None, :] - positions[:, None])
    cycle_dist = jnp.minimum(apart, total_angles - apart)
    hit = jnp.where(cycle_dist < a_dev, -LOAD, 0.0)
    select = jnp.where(lax.iota(jnp.int32, comps) == 2, 1.0, 0.0)
    right = loads + hit[:, None, :, None, None] * select[None, :, None, None, None]

    def precondition(r):
        coarse_rhs = restrict(r)
        err = OMEGA * coarse_rhs / diag_c
        for sweep in range(CSWEEPS - 1):
            err = err + OMEGA * (coarse_rhs - split_apply(err, wide_c, spring_c)) / diag_c
        return OMEGA * r / diag + prolong(err)

    def projection(a, b):
        return lax.psum(jnp.sum(a * b, axis=(2, 3, 4)), ("ang", "hgt"))[:, :, None, None, None]

    solution_field = jnp.zeros_like(right)
    residual = right
    precond = precondition(residual)
    direction = precond
    rz_now = projection(residual, precond)
    for step in range(ITERS):
        image = fine_apply(direction, weight, spring)
        curve = lax.psum(jnp.sum(direction * image, axis=(2, 3, 4)), ("ang", "hgt"))
        alpha = rz_now / curve[:, :, None, None, None]
        solution_field = solution_field + alpha * direction
        residual = residual - alpha * image
        if step + 1 < ITERS:
            precond = precondition(residual)
            rz_next = projection(residual, precond)
            direction = precond + rz_next / rz_now * direction
            rz_now = rz_next
    return (solution_field, residual)


def solution(mesh):
    in_specs = (
        P(None, None, "ang", "hgt", None),
        P("ang", "hgt", None),
        P("ang", "hgt", None),
        P(),
        P(),
    )
    out_specs = (P(None, None, "ang", "hgt", None), P(None, None, "ang", "hgt", None))
    return jax.shard_map(body, mesh=mesh, in_specs=in_specs, out_specs=out_specs, check_vma=False)
```

profile of v0, /device:TPU:1, one launch (start us, length us, event | category | flops | bytes accessed | tf_op | source)
XLA Modules:
  0.0 547.7 jit_solution(10742508094676657022)
XLA Ops:
  9.7 4.7 collective-permute-start.3
  18.5 3.0 collective-permute-done.1
  23.3 4.0 collective-permute-start.7
  27.4 6.8 %collective-permute-start.4 = (f32[4,3,1,4,128]{4,2,3,1,0:T(1,128)S(1)}, f32[4,3,1,4,128]{4,2,3,1,0:T(1,128)S(1)}, u32[]{:S(2)}, u32[]{:S(2)}) collective-permute-start(f32[4,3,1,4,128]{4,2,3,1,0:T(1,128)S(1)} %get-tuple-element.77), channel_id=1, source_target_pairs={{8,0},{16,8},{24,16},{32,24},{40,32},{48,40},{56,48},{64,56},{72,6... | collective-permute-start | bytes 73736 | tf_op jit(solution)/shard_map/ppermute | solution.py:26
  37.1 4.0 collective-permute-start.11
  41.2 6.4 %collective-permute-start.8 = (f32[4,3,1,4,128]{4,2,3,1,0:T(1,128)S(1)}, f32[4,3,1,4,128]{4,2,3,1,0:T(1,128)S(1)}, u32[]{:S(2)}, u32[]{:S(2)}) collective-permute-start(f32[4,3,1,4,128]{4,2,3,1,0:T(1,128)S(1)} %get-tuple-element.73), channel_id=1, source_target_pairs={{8,0},{16,8},{24,16},{32,24},{40,32},{48,40},{56,48},{64,56},{72,6... | collective-permute-start | bytes 73736 | tf_op jit(solution)/shard_map/ppermute | solution.py:26
  52.6 4.8 collective-permute-start.15
  57.5 6.1 %collective-permute-start.12 = (f32[4,3,1,8,128]{4,2,3,1,0:T(1,128)S(1)}, f32[4,3,1,8,128]{4,2,3,1,0:T(1,128)S(1)}, u32[]{:S(2)}, u32[]{:S(2)}) collective-permute-start(f32[4,3,1,8,128]{4,2,3,1,0:T(1,128)S(1)} %get-tuple-element.45), channel_id=1, source_target_pairs={{8,0},{16,8},{24,16},{32,24},{40,32},{48,40},{56,48},{64,56},{72,6... | collective-permute-start | bytes 147464 | tf_op jit(solution)/shard_map/ppermute | solution.py:26
  64.8 3.0 multiply_reduce_fusion.4
  67.9 75.8 %all-reduce.12 = (f32[4,3]{1,0:T(4,128)S(1)}, f32[4,3]{1,0:T(4,128)S(1)}) all-reduce(f32[4,3]{1,0:T(4,128)S(1)} %get-tuple-element.11, f32[4,3]{1,0:T(4,128)S(1)} %get-tuple-element.10), channel_id=1, replica_groups=mesh['ang'=16,'hgt'=8] {'ang','hgt'}, use_global_device_ids=true, to_apply=%region_5.6 | all-reduce | flops 24 | bytes 192 | tf_op jit(solution)/shard_map/psum | solution.py:102
  148.2 4.0 collective-permute-start.19
  158.4 4.0 collective-permute-start.23
  162.5 6.8 %collective-permute-start.20 = (f32[4,3,1,4,128]{4,2,3,1,0:T(1,128)S(1)}, f32[4,3,1,4,128]{4,2,3,1,0:T(1,128)S(1)}, u32[]{:S(2)}, u32[]{:S(2)}) collective-permute-start(f32[4,3,1,4,128]{4,2,3,1,0:T(1,128)S(1)} %get-tuple-element.65), channel_id=1, source_target_pairs={{8,0},{16,8},{24,16},{32,24},{40,32},{48,40},{56,48},{64,56},{72,6... | collective-permute-start | bytes 73736 | tf_op jit(solution)/shard_map/ppermute | solution.py:26
  172.2 4.0 collective-permute-start.27
  176.3 6.4 %collective-permute-start.24 = (f32[4,3,1,4,128]{4,2,3,1,0:T(1,128)S(1)}, f32[4,3,1,4,128]{4,2,3,1,0:T(1,128)S(1)}, u32[]{:S(2)}, u32[]{:S(2)}) collective-permute-start(f32[4,3,1,4,128]{4,2,3,1,0:T(1,128)S(1)} %get-tuple-element.61), channel_id=1, source_target_pairs={{8,0},{16,8},{24,16},{32,24},{40,32},{48,40},{56,48},{64,56},{72,6... | collective-permute-start | bytes 73736 | tf_op jit(solution)/shard_map/ppermute | solution.py:26
  186.5 71.3 %psum.44 = f32[4,3]{1,0:T(4,128)S(1)} all-reduce(f32[4,3]{1,0:T(4,128)S(1)} %multiply_reduce_fusion.3), channel_id=1, replica_groups=mesh['ang'=16,'hgt'=8] {'ang','hgt'}, use_global_device_ids=true, to_apply=%region_10.11 | all-reduce | flops 12 | bytes 96 | tf_op jit(solution)/shard_map/psum | solution.py:102
  261.4 4.0 collective-permute-start.31
  270.4 2.7 multiply_reduce_fusion.2
  273.1 68.5 %psum.45 = f32[4,3]{1,0:T(4,128)S(1)} all-reduce(f32[4,3]{1,0:T(4,128)S(1)} %get-tuple-element.22), channel_id=1, replica_groups=mesh['ang'=16,'hgt'=8] {'ang','hgt'}, use_global_device_ids=true, to_apply=%region_12.13 | all-reduce | flops 12 | bytes 96 | tf_op jit(solution)/shard_map/psum | solution.py:111
  346.1 4.0 collective-permute-start.35
  356.0 4.0 collective-permute-start.39
  360.0 6.8 %collective-permute-start.36 = (f32[4,3,1,4,128]{4,2,3,1,0:T(1,128)S(1)}, f32[4,3,1,4,128]{4,2,3,1,0:T(1,128)S(1)}, u32[]{:S(2)}, u32[]{:S(2)}) collective-permute-start(f32[4,3,1,4,128]{4,2,3,1,0:T(1,128)S(1)} %get-tuple-element.53), channel_id=1, source_target_pairs={{8,0},{16,8},{24,16},{32,24},{40,32},{48,40},{56,48},{64,56},{72,6... | collective-permute-start | bytes 73736 | tf_op jit(solution)/shard_map/ppermute | solution.py:26
  369.8 4.0 collective-permute-start.43
  373.9 6.4 %collective-permute-start.40 = (f32[4,3,1,4,128]{4,2,3,1,0:T(1,128)S(1)}, f32[4,3,1,4,128]{4,2,3,1,0:T(1,128)S(1)}, u32[]{:S(2)}, u32[]{:S(2)}) collective-permute-start(f32[4,3,1,4,128]{4,2,3,1,0:T(1,128)S(1)} %get-tuple-element.49), channel_id=1, source_target_pairs={{8,0},{16,8},{24,16},{32,24},{40,32},{48,40},{56,48},{64,56},{72,6... | collective-permute-start | bytes 73736 | tf_op jit(solution)/shard_map/ppermute | solution.py:26
  384.1 71.3 %psum.46 = f32[4,3]{1,0:T(4,128)S(1)} all-reduce(f32[4,3]{1,0:T(4,128)S(1)} %multiply_reduce_fusion.1), channel_id=1, replica_groups=mesh['ang'=16,'hgt'=8] {'ang','hgt'}, use_global_device_ids=true, to_apply=%region_15.16 | all-reduce | flops 12 | bytes 96 | tf_op jit(solution)/shard_map/psum | solution.py:102
  455.4 2.2 broadcast_multiply_fusion
  459.0 4.0 collective-permute-start.47
  468.1 2.7 multiply_reduce_fusion
  470.8 68.6 %psum.47 = f32[4,3]{1,0:T(4,128)S(1)} all-reduce(f32[4,3]{1,0:T(4,128)S(1)} %get-tuple-element.14), channel_id=1, replica_groups=mesh['ang'=16,'hgt'=8] {'ang','hgt'}, use_global_device_ids=true, to_apply=%region_17.18 | all-reduce | flops 12 | bytes 96 | tf_op jit(solution)/shard_map/psum | solution.py:111
  539.4 3.4 multiply_subtract_fusion
  542.8 2.2 copy.39
  545.0 2.2 copy.38
  (170 shorter events, 73.7 us)
Async XLA Ops:
  8.4 13.1 %collective-permute-start.2 = (f32[4,3,16,1,128]{4,2,3,1,0:T(8,128)S(1)}, f32[4,3,16,1,128]{4,2,3,1,0:T(8,128)S(1)}, u32[]{:S(2)}, u32[]{:S(2)}) collective-permute-start(f32[4,3,16,1,128]{4,2,3,1,0:T(8,128)S(1)} %get-tuple-element.83), channel_id=1, source_target_pairs={{1,0},{2,1},{3,2},{4,3},{5,4},{6,5},{7,6},{9,8},{10,9},{11,10},{12... | collective-permute-start | bytes 294920 | tf_op jit(solution)/shard_map/ppermute | solution.py:26
  9.7 11.8 %collective-permute-start.3 = (f32[4,3,16,1,128]{4,2,3,1,0:T(8,128)S(1)}, f32[4,3,16,1,128]{4,2,3,1,0:T(8,128)S(1)}, u32[]{:S(2)}, u32[]{:S(2)}) collective-permute-start(f32[4,3,16,1,128]{4,2,3,1,0:T(8,128)S(1)} %get-tuple-element.84), channel_id=1, source_target_pairs={{0,1},{1,2},{2,3},{3,4},{4,5},{5,6},{6,7},{8,9},{9,10},{10,11},{11... | collective-permute-start | bytes 294920 | tf_op jit(solution)/shard_map/ppermute | solution.py:23
  15.8 5.8 %collective-permute-start.1 = (f32[4,3,1,4,128]{4,2,3,1,0:T(1,128)S(1)}, f32[4,3,1,4,128]{4,2,3,1,0:T(1,128)S(1)}, u32[]{:S(2)}, u32[]{:S(2)}) collective-permute-start(f32[4,3,1,4,128]{4,2,3,1,0:T(1,128)S(1)} %get-tuple-element.82), channel_id=1, source_target_pairs={{0,8},{8,16},{16,24},{24,32},{32,40},{40,48},{48,56},{56,64},{64,7... | collective-permute-start | bytes 73736 | tf_op jit(solution)/shard_map/ppermute | solution.py:23
  22.0 13.3 %collective-permute-start.6 = (f32[4,3,16,1,128]{4,2,3,1,0:T(8,128)S(1)}, f32[4,3,16,1,128]{4,2,3,1,0:T(8,128)S(1)}, u32[]{:S(2)}, u32[]{:S(2)}) collective-permute-start(f32[4,3,16,1,128]{4,2,3,1,0:T(8,128)S(1)} %get-tuple-element.79), channel_id=1, source_target_pairs={{1,0},{2,1},{3,2},{4,3},{5,4},{6,5},{7,6},{9,8},{10,9},{11,10},{12... | collective-permute-start | bytes 294920 | tf_op jit(solution)/shard_map/ppermute | solution.py:26
  23.3 12.1 %collective-permute-start.7 = (f32[4,3,16,1,128]{4,2,3,1,0:T(8,128)S(1)}, f32[4,3,16,1,128]{4,2,3,1,0:T(8,128)S(1)}, u32[]{:S(2)}, u32[]{:S(2)}) collective-permute-start(f32[4,3,16,1,128]{4,2,3,1,0:T(8,128)S(1)} %get-tuple-element.80), channel_id=1, source_target_pairs={{0,1},{1,2},{2,3},{3,4},{4,5},{5,6},{6,7},{8,9},{9,10},{10,11},{11... | collective-permute-start | bytes 294920 | tf_op jit(solution)/shard_map/ppermute | solution.py:23
  27.4 7.7 %collective-permute-start.4 = (f32[4,3,1,4,128]{4,2,3,1,0:T(1,128)S(1)}, f32[4,3,1,4,128]{4,2,3,1,0:T(1,128)S(1)}, u32[]{:S(2)}, u32[]{:S(2)}) collective-permute-start(f32[4,3,1,4,128]{4,2,3,1,0:T(1,128)S(1)} %get-tuple-element.77), channel_id=1, source_target_pairs={{8,0},{16,8},{24,16},{32,24},{40,32},{48,40},{56,48},{64,56},{72,6... | collective-permute-start | bytes 73736 | tf_op jit(solution)/shard_map/ppermute | solution.py:26
  35.8 12.9 %collective-permute-start.10 = (f32[4,3,16,1,128]{4,2,3,1,0:T(8,128)S(1)}, f32[4,3,16,1,128]{4,2,3,1,0:T(8,128)S(1)}, u32[]{:S(2)}, u32[]{:S(2)}) collective-permute-start(f32[4,3,16,1,128]{4,2,3,1,0:T(8,128)S(1)} %get-tuple-element.75), channel_id=1, source_target_pairs={{1,0},{2,1},{3,2},{4,3},{5,4},{6,5},{7,6},{9,8},{10,9},{11,10},{12... | collective-permute-start | bytes 294920 | tf_op jit(solution)/shard_map/ppermute | solution.py:26
  37.1 11.6 %collective-permute-start.11 = (f32[4,3,16,1,128]{4,2,3,1,0:T(8,128)S(1)}, f32[4,3,16,1,128]{4,2,3,1,0:T(8,128)S(1)}, u32[]{:S(2)}, u32[]{:S(2)}) collective-permute-start(f32[4,3,16,1,128]{4,2,3,1,0:T(8,128)S(1)} %get-tuple-element.76), channel_id=1, source_target_pairs={{0,1},{1,2},{2,3},{3,4},{4,5},{5,6},{6,7},{8,9},{9,10},{10,11},{11... | collective-permute-start | bytes 294920 | tf_op jit(solution)/shard_map/ppermute | solution.py:23
  41.2 7.2 %collective-permute-start.8 = (f32[4,3,1,4,128]{4,2,3,1,0:T(1,128)S(1)}, f32[4,3,1,4,128]{4,2,3,1,0:T(1,128)S(1)}, u32[]{:S(2)}, u32[]{:S(2)}) collective-permute-start(f32[4,3,1,4,128]{4,2,3,1,0:T(1,128)S(1)} %get-tuple-element.73), channel_id=1, source_target_pairs={{8,0},{16,8},{24,16},{32,24},{40,32},{48,40},{56,48},{64,56},{72,6... | collective-permute-start | bytes 73736 | tf_op jit(solution)/shard_map/ppermute | solution.py:26
  51.3 13.5 %collective-permute-start.14 = (f32[4,3,32,1,128]{4,2,3,1,0:T(8,128)S(1)}, f32[4,3,32,1,128]{4,2,3,1,0:T(8,128)S(1)}, u32[]{:S(2)}, u32[]{:S(2)}) collective-permute-start(f32[4,3,32,1,128]{4,2,3,1,0:T(8,128)S(1)} %get-tuple-element.47), channel_id=1, source_target_pairs={{1,0},{2,1},{3,2},{4,3},{5,4},{6,5},{7,6},{9,8},{10,9},{11,10},{12... | collective-permute-start | bytes 589832 | tf_op jit(solution)/shard_map/ppermute | solution.py:26
  52.6 12.2 %collective-permute-start.15 = (f32[4,3,32,1,128]{4,2,3,1,0:T(8,128)S(1)}, f32[4,3,32,1,128]{4,2,3,1,0:T(8,128)S(1)}, u32[]{:S(2)}, u32[]{:S(2)}) collective-permute-start(f32[4,3,32,1,128]{4,2,3,1,0:T(8,128)S(1)} %get-tuple-element.48), channel_id=1, source_target_pairs={{0,1},{1,2},{2,3},{3,4},{4,5},{5,6},{6,7},{8,9},{9,10},{10,11},{11... | collective-permute-start | bytes 589832 | tf_op jit(solution)/shard_map/ppermute | solution.py:23
  57.5 7.0 %collective-permute-start.12 = (f32[4,3,1,8,128]{4,2,3,1,0:T(1,128)S(1)}, f32[4,3,1,8,128]{4,2,3,1,0:T(1,128)S(1)}, u32[]{:S(2)}, u32[]{:S(2)}) collective-permute-start(f32[4,3,1,8,128]{4,2,3,1,0:T(1,128)S(1)} %get-tuple-element.45), channel_id=1, source_target_pairs={{8,0},{16,8},{24,16},{32,24},{40,32},{48,40},{56,48},{64,56},{72,6... | collective-permute-start | bytes 147464 | tf_op jit(solution)/shard_map/ppermute | solution.py:26
  146.9 9.8 %collective-permute-start.18 = (f32[4,3,16,1,128]{4,2,3,1,0:T(8,128)S(1)}, f32[4,3,16,1,128]{4,2,3,1,0:T(8,128)S(1)}, u32[]{:S(2)}, u32[]{:S(2)}) collective-permute-start(f32[4,3,16,1,128]{4,2,3,1,0:T(8,128)S(1)} %get-tuple-element.71), channel_id=1, source_target_pairs={{1,0},{2,1},{3,2},{4,3},{5,4},{6,5},{7,6},{9,8},{10,9},{11,10},{12... | collective-permute-start | bytes 294920 | tf_op jit(solution)/shard_map/ppermute | solution.py:26
  148.2 8.5 %collective-permute-start.19 = (f32[4,3,16,1,128]{4,2,3,1,0:T(8,128)S(1)}, f32[4,3,16,1,128]{4,2,3,1,0:T(8,128)S(1)}, u32[]{:S(2)}, u32[]{:S(2)}) collective-permute-start(f32[4,3,16,1,128]{4,2,3,1,0:T(8,128)S(1)} %get-tuple-element.72), channel_id=1, source_target_pairs={{0,1},{1,2},{2,3},{3,4},{4,5},{5,6},{6,7},{8,9},{9,10},{10,11},{11... | collective-permute-start | bytes 294920 | tf_op jit(solution)/shard_map/ppermute | solution.py:23
  157.1 13.3 %collective-permute-start.22 = (f32[4,3,16,1,128]{4,2,3,1,0:T(8,128)S(1)}, f32[4,3,16,1,128]{4,2,3,1,0:T(8,128)S(1)}, u32[]{:S(2)}, u32[]{:S(2)}) collective-permute-start(f32[4,3,16,1,128]{4,2,3,1,0:T(8,128)S(1)} %get-tuple-element.67), channel_id=1, source_target_pairs={{1,0},{2,1},{3,2},{4,3},{5,4},{6,5},{7,6},{9,8},{10,9},{11,10},{12... | collective-permute-start | bytes 294920 | tf_op jit(solution)/shard_map/ppermute | solution.py:26
  158.4 12.1 %collective-permute-start.23 = (f32[4,3,16,1,128]{4,2,3,1,0:T(8,128)S(1)}, f32[4,3,16,1,128]{4,2,3,1,0:T(8,128)S(1)}, u32[]{:S(2)}, u32[]{:S(2)}) collective-permute-start(f32[4,3,16,1,128]{4,2,3,1,0:T(8,128)S(1)} %get-tuple-element.68), channel_id=1, source_target_pairs={{0,1},{1,2},{2,3},{3,4},{4,5},{5,6},{6,7},{8,9},{9,10},{10,11},{11... | collective-permute-start | bytes 294920 | tf_op jit(solution)/shard_map/ppermute | solution.py:23
  162.5 7.7 %collective-permute-start.20 = (f32[4,3,1,4,128]{4,2,3,1,0:T(1,128)S(1)}, f32[4,3,1,4,128]{4,2,3,1,0:T(1,128)S(1)}, u32[]{:S(2)}, u32[]{:S(2)}) collective-permute-start(f32[4,3,1,4,128]{4,2,3,1,0:T(1,128)S(1)} %get-tuple-element.65), channel_id=1, source_target_pairs={{8,0},{16,8},{24,16},{32,24},{40,32},{48,40},{56,48},{64,56},{72,6... | collective-permute-start | bytes 73736 | tf_op jit(solution)/shard_map/ppermute | solution.py:26
  170.9 12.9 %collective-permute-start.26 = (f32[4,3,16,1,128]{4,2,3,1,0:T(8,128)S(1)}, f32[4,3,16,1,128]{4,2,3,1,0:T(8,128)S(1)}, u32[]{:S(2)}, u32[]{:S(2)}) collective-permute-start(f32[4,3,16,1,128]{4,2,3,1,0:T(8,128)S(1)} %get-tuple-element.63), channel_id=1, source_target_pairs={{1,0},{2,1},{3,2},{4,3},{5,4},{6,5},{7,6},{9,8},{10,9},{11,10},{12... | collective-permute-start | bytes 294920 | tf_op jit(solution)/shard_map/ppermute | solution.py:26
  172.2 11.6 %collective-permute-start.27 = (f32[4,3,16,1,128]{4,2,3,1,0:T(8,128)S(1)}, f32[4,3,16,1,128]{4,2,3,1,0:T(8,128)S(1)}, u32[]{:S(2)}, u32[]{:S(2)}) collective-permute-start(f32[4,3,16,1,128]{4,2,3,1,0:T(8,128)S(1)} %get-tuple-element.64), channel_id=1, source_target_pairs={{0,1},{1,2},{2,3},{3,4},{4,5},{5,6},{6,7},{8,9},{9,10},{10,11},{11... | collective-permute-start | bytes 294920 | tf_op jit(solution)/shard_map/ppermute | solution.py:23
  176.3 7.2 %collective-permute-start.24 = (f32[4,3,1,4,128]{4,2,3,1,0:T(1,128)S(1)}, f32[4,3,1,4,128]{4,2,3,1,0:T(1,128)S(1)}, u32[]{:S(2)}, u32[]{:S(2)}) collective-permute-start(f32[4,3,1,4,128]{4,2,3,1,0:T(1,128)S(1)} %get-tuple-element.61), channel_id=1, source_target_pairs={{8,0},{16,8},{24,16},{32,24},{40,32},{48,40},{56,48},{64,56},{72,6... | collective-permute-start | bytes 73736 | tf_op jit(solution)/shard_map/ppermute | solution.py:26
  260.1 10.3 %collective-permute-start.30 = (f32[4,3,32,1,128]{4,2,3,1,0:T(8,128)S(1)}, f32[4,3,32,1,128]{4,2,3,1,0:T(8,128)S(1)}, u32[]{:S(2)}, u32[]{:S(2)}) collective-permute-start(f32[4,3,32,1,128]{4,2,3,1,0:T(8,128)S(1)} %get-tuple-element.43), channel_id=1, source_target_pairs={{1,0},{2,1},{3,2},{4,3},{5,4},{6,5},{7,6},{9,8},{10,9},{11,10},{12... | collective-permute-start | bytes 589832 | tf_op jit(solution)/shard_map/ppermute | solution.py:26
  261.4 9.0 %collective-permute-start.31 = (f32[4,3,32,1,128]{4,2,3,1,0:T(8,128)S(1)}, f32[4,3,32,1,128]{4,2,3,1,0:T(8,128)S(1)}, u32[]{:S(2)}, u32[]{:S(2)}) collective-permute-start(f32[4,3,32,1,128]{4,2,3,1,0:T(8,128)S(1)} %get-tuple-element.44), channel_id=1, source_target_pairs={{0,1},{1,2},{2,3},{3,4},{4,5},{5,6},{6,7},{8,9},{9,10},{10,11},{11... | collective-permute-start | bytes 589832 | tf_op jit(solution)/shard_map/ppermute | solution.py:23
  344.8 9.4 %collective-permute-start.34 = (f32[4,3,16,1,128]{4,2,3,1,0:T(8,128)S(1)}, f32[4,3,16,1,128]{4,2,3,1,0:T(8,128)S(1)}, u32[]{:S(2)}, u32[]{:S(2)}) collective-permute-start(f32[4,3,16,1,128]{4,2,3,1,0:T(8,128)S(1)} %get-tuple-element.59), channel_id=1, source_target_pairs={{1,0},{2,1},{3,2},{4,3},{5,4},{6,5},{7,6},{9,8},{10,9},{11,10},{12... | collective-permute-start | bytes 294920 | tf_op jit(solution)/shard_map/ppermute | solution.py:26
  346.1 8.1 %collective-permute-start.35 = (f32[4,3,16,1,128]{4,2,3,1,0:T(8,128)S(1)}, f32[4,3,16,1,128]{4,2,3,1,0:T(8,128)S(1)}, u32[]{:S(2)}, u32[]{:S(2)}) collective-permute-start(f32[4,3,16,1,128]{4,2,3,1,0:T(8,128)S(1)} %get-tuple-element.60), channel_id=1, source_target_pairs={{0,1},{1,2},{2,3},{3,4},{4,5},{5,6},{6,7},{8,9},{9,10},{10,11},{11... | collective-permute-start | bytes 294920 | tf_op jit(solution)/shard_map/ppermute | solution.py:23
  354.7 13.3 %collective-permute-start.38 = (f32[4,3,16,1,128]{4,2,3,1,0:T(8,128)S(1)}, f32[4,3,16,1,128]{4,2,3,1,0:T(8,128)S(1)}, u32[]{:S(2)}, u32[]{:S(2)}) collective-permute-start(f32[4,3,16,1,128]{4,2,3,1,0:T(8,128)S(1)} %get-tuple-element.55), channel_id=1, source_target_pairs={{1,0},{2,1},{3,2},{4,3},{5,4},{6,5},{7,6},{9,8},{10,9},{11,10},{12... | collective-permute-start | bytes 294920 | tf_op jit(solution)/shard_map/ppermute | solution.py:26
  356.0 12.1 %collective-permute-start.39 = (f32[4,3,16,1,128]{4,2,3,1,0:T(8,128)S(1)}, f32[4,3,16,1,128]{4,2,3,1,0:T(8,128)S(1)}, u32[]{:S(2)}, u32[]{:S(2)}) collective-permute-start(f32[4,3,16,1,128]{4,2,3,1,0:T(8,128)S(1)} %get-tuple-element.56), channel_id=1, source_target_pairs={{0,1},{1,2},{2,3},{3,4},{4,5},{5,6},{6,7},{8,9},{9,10},{10,11},{11... | collective-permute-start | bytes 294920 | tf_op jit(solution)/shard_map/ppermute | solution.py:23
  360.0 7.7 %collective-permute-start.36 = (f32[4,3,1,4,128]{4,2,3,1,0:T(1,128)S(1)}, f32[4,3,1,4,128]{4,2,3,1,0:T(1,128)S(1)}, u32[]{:S(2)}, u32[]{:S(2)}) collective-permute-start(f32[4,3,1,4,128]{4,2,3,1,0:T(1,128)S(1)} %get-tuple-element.53), channel_id=1, source_target_pairs={{8,0},{16,8},{24,16},{32,24},{40,32},{48,40},{56,48},{64,56},{72,6... | collective-permute-start | bytes 73736 | tf_op jit(solution)/shard_map/ppermute | solution.py:26
  368.5 12.9 %collective-permute-start.42 = (f32[4,3,16,1,128]{4,2,3,1,0:T(8,128)S(1)}, f32[4,3,16,1,128]{4,2,3,1,0:T(8,128)S(1)}, u32[]{:S(2)}, u32[]{:S(2)}) collective-permute-start(f32[4,3,16,1,128]{4,2,3,1,0:T(8,128)S(1)} %get-tuple-element.51), channel_id=1, source_target_pairs={{1,0},{2,1},{3,2},{4,3},{5,4},{6,5},{7,6},{9,8},{10,9},{11,10},{12... | collective-permute-start | bytes 294920 | tf_op jit(solution)/shard_map/ppermute | solution.py:26
  369.8 11.6 %collective-permute-start.43 = (f32[4,3,16,1,128]{4,2,3,1,0:T(8,128)S(1)}, f32[4,3,16,1,128]{4,2,3,1,0:T(8,128)S(1)}, u32[]{:S(2)}, u32[]{:S(2)}) collective-permute-start(f32[4,3,16,1,128]{4,2,3,1,0:T(8,128)S(1)} %get-tuple-element.52), channel_id=1, source_target_pairs={{0,1},{1,2},{2,3},{3,4},{4,5},{5,6},{6,7},{8,9},{9,10},{10,11},{11... | collective-permute-start | bytes 294920 | tf_op jit(solution)/shard_map/ppermute | solution.py:23
  373.9 7.2 %collective-permute-start.40 = (f32[4,3,1,4,128]{4,2,3,1,0:T(1,128)S(1)}, f32[4,3,1,4,128]{4,2,3,1,0:T(1,128)S(1)}, u32[]{:S(2)}, u32[]{:S(2)}) collective-permute-start(f32[4,3,1,4,128]{4,2,3,1,0:T(1,128)S(1)} %get-tuple-element.49), channel_id=1, source_target_pairs={{8,0},{16,8},{24,16},{32,24},{40,32},{48,40},{56,48},{64,56},{72,6... | collective-permute-start | bytes 73736 | tf_op jit(solution)/shard_map/ppermute | solution.py:26
  457.7 10.4 %collective-permute-start.46 = (f32[4,3,32,1,128]{4,2,3,1,0:T(8,128)S(1)}, f32[4,3,32,1,128]{4,2,3,1,0:T(8,128)S(1)}, u32[]{:S(2)}, u32[]{:S(2)}) collective-permute-start(f32[4,3,32,1,128]{4,2,3,1,0:T(8,128)S(1)} %get-tuple-element.39), channel_id=1, source_target_pairs={{1,0},{2,1},{3,2},{4,3},{5,4},{6,5},{7,6},{9,8},{10,9},{11,10},{12... | collective-permute-start | bytes 589832 | tf_op jit(solution)/shard_map/ppermute | solution.py:26
  459.0 9.1 %collective-permute-start.47 = (f32[4,3,32,1,128]{4,2,3,1,0:T(8,128)S(1)}, f32[4,3,32,1,128]{4,2,3,1,0:T(8,128)S(1)}, u32[]{:S(2)}, u32[]{:S(2)}) collective-permute-start(f32[4,3,32,1,128]{4,2,3,1,0:T(8,128)S(1)} %get-tuple-element.40), channel_id=1, source_target_pairs={{0,1},{1,2},{2,3},{3,4},{4,5},{5,6},{6,7},{8,9},{9,10},{10,11},{11... | collective-permute-start | bytes 589832 | tf_op jit(solution)/shard_map/ppermute | solution.py:23
  (28 other events, 275.4 us)
where the time goes:
time: 556 us; the launch traced here: 548 us
  blocking collectives  356 us (64%)
  starting transfers between devices  124 us (22%)
  other arithmetic  35.7 us (6%)
  waiting for transfers between devices  20.6 us (4%)
  local copies, waits for them, and re-layouts  10.2 us (2%)
    psum x3, blocking collectives, projection(): lax.psum(jnp.sum(a * b, axis=(2, 3, 4)), ('ang', 'hgt'))  218 us
    psum x2, blocking collectives, body(): curve = lax.psum(jnp.sum(direction * image, axis=(2, 3, 4)), ('ang', 'hgt'))  137 us
    ppermute x24, starting transfers between devices, padded_2(): lax.ppermute(lax.slice_in_dim(block, 0, width, axis=dim), axis, backward)  67.4 us
    ppermute x24, starting transfers between devices, padded_2(): lax.ppermute(lax.slice_in_dim(block, block.shape[dim] - width, None, axis...  56.4 us
    ppermute x24, waiting for transfers between devices, padded_2(): lax.ppermute(lax.slice_in_dim(block, 0, width, axis=dim), axis, backward)  13.5 us
  transfers between devices with their start and end apart: 48, of which 24 were waited for; matrix products, arithmetic and copies ran while one was open for 0% of the time, Pallas kernels for 0%

commit v1 on v0

v1 whole, which is shorter than its diff:
```python
import functools

import jax
import jax.numpy as jnp
from jax import lax
from jax.experimental import pallas as pl
from jax.experimental.pallas import tpu as pltpu
from jax.sharding import PartitionSpec as P

STEPS = 3
SIGMA = 6.5
SPRING = 20.0
OMEGA = 0.8
LOAD = 3.0
GROUPS = 3
MESH = pl.DeviceIdType.MESH
F32 = jnp.float32
T = (8, 128)
UP, DOWN, RIGHT, LEFT, RU, LU, RD, LD = range(8)
SHIFT = ((0, 1), (0, -1), (1, 0), (-1, 0), (1, 1), (-1, 1), (1, -1), (-1, -1))


def kernel(
    modulus, positions, loads, material, support,
    out_x, out_r,
    mat, sup, weight, spring, diag, kf, kv, iw,
    res, ys, vf, pe, co, sr, sl, sc, hl, hr, rc, pr, ring,
    fsu, fsd, fu, fd, fl, fr, tsum, pa, pb,
    in_sem, dsend, drecv, fsend, frecv, psend, precv, out_sem,
):
    na, nh = lax.axis_size("ang"), lax.axis_size("hgt")
    me_a, me_h = lax.axis_index("ang"), lax.axis_index("hgt")
    cols = loads.shape[0]
    groups = GROUPS
    per = cols // groups
    pcol = cols
    angs = 32
    sub = lax.broadcasted_iota(jnp.int32, T, 0)
    lane = lax.broadcasted_iota(jnp.int32, T, 1)
    has_up, has_down = me_h < nh - 1, me_h > 0

    def device(da, dh):
        return {"ang": lax.rem(me_a + da + na, na), "hgt": me_h + dh}

    def guarded(dh, body):
        if dh > 0:
            pl.when(has_up)(body)
        elif dh < 0:
            pl.when(has_down)(body)
        else:
            body()

    in_copies = [pltpu.make_async_copy(material, mat, in_sem.at[groups]),
                 pltpu.make_async_copy(support, sup, in_sem.at[groups + 1])]
    for copy in in_copies:
        copy.start()

    def load_copy(g):
        c = pl.ds(g * per, per)
        return pltpu.make_async_copy(loads.at[c], res.at[0, c], in_sem.at[g])

    for g in range(groups):
        load_copy(g).start()

    barrier = pltpu.get_barrier_semaphore()

    def greet_a(d, carry):
        pl.semaphore_signal(barrier, inc=1, device_id={"ang": lax.rem(me_a + d, na), "hgt": me_h}, device_id_type=MESH)
        return carry

    def greet_h(d, carry):
        pl.semaphore_signal(barrier, inc=1, device_id={"ang": me_a, "hgt": lax.rem(me_h + d, nh)}, device_id_type=MESH)
        return carry

    for da, dh in SHIFT[4:]:
        guarded(dh, lambda da=da, dh=dh: pl.semaphore_signal(
            barrier, inc=1, device_id=device(da, dh), device_id_type=MESH))
    lax.fori_loop(1, na, greet_a, 0)
    lax.fori_loop(1, nh, greet_h, 0)

    def roll(x, shift, axis=0):
        return pltpu.roll(x, shift % x.shape[axis], axis)

    def lanes(v):
        return jnp.where(lane == 0, 0.0, roll(v, 1, 1)) + jnp.where(lane == 127, 0.0, roll(v, -1, 1))

    def quad(ref, j, b, *lead):
        total = None
        for da in range(2):
            for dh in range(2):
                part = ref[(*lead, pl.ds(b * 128 + da * 8 + 2 * j + dh, 8, stride=16), slice(None))]
                total = part if total is None else total + part
        return total

    zero = jnp.zeros(T, F32)

    def clear(row, corners, fine):
        def one(c, carry):
            for k in range(STEPS):
                for j in range(3):
                    for b in range(2):
                        co[k, c, row + j, pl.ds(8 * b, 8), :] = zero
            return carry

        lax.fori_loop(0, cols + 1, one, 0)

        def two(c, carry):
            for k in range(STEPS):
                for i in range(4):
                    fine[k, c, pl.ds(8 * i, 8), :] = zero
            return carry

        lax.fori_loop(0, cols, two, 0)

        def three(c, carry):
            for k in range(STEPS):
                for d in corners:
                    rc[k, d, c] = zero
            return carry

        lax.fori_loop(0, cols // 2 + 1, three, 0)

    pl.when(jnp.logical_not(has_down))(lambda: clear(0, (RU - 4, LU - 4), fd))
    pl.when(jnp.logical_not(has_up))(lambda: clear(7, (RD - 4, LD - 4), fu))

    def deep(k, slot, first, count, d):
        c = pl.ds(first, count)
        pair = pl.ds(first // 2, (count + 1) // 2)
        if d == UP:
            src, dst = co.at[k, c, pl.ds(4, 3)], co.at[k, c, pl.ds(0, 3)]
        elif d == DOWN:
            src, dst = co.at[k, c, pl.ds(3, 3)], co.at[k, c, pl.ds(7, 3)]
        elif d == RIGHT:
            src, dst = sr.at[c], hl.at[k, c]
        elif d == LEFT:
            src, dst = sl.at[c], hr.at[k, c]
        else:
            src, dst = sc.at[d - 4, pair], rc.at[k, d - 4, pair]
        return pltpu.make_async_remote_copy(
            src_ref=src, dst_ref=dst, send_sem=dsend.at[k, slot, d], recv_sem=drecv.at[k, slot, d],
            device_id=device(*SHIFT[d]), device_id_type=MESH)

    def deep_start(k, slot, first, count):
        for d in (UP, DOWN, RU, LU, RD, LD, RIGHT, LEFT):
            guarded(SHIFT[d][1], lambda d=d: deep(k, slot, first, count, d).start())

    def deep_wait(k, slot, first, count):
        for d in range(8):
            guarded(SHIFT[d][1], lambda d=d: deep(k, slot, first, count, d).wait_send())
            guarded(-SHIFT[d][1], lambda d=d: deep(k, slot, first, count, d).wait_recv())

    def fine(k, g, d):
        c = pl.ds(g * per, per)
        if d == UP:
            src, dst = fsu.at[c], fd.at[k, c]
        elif d == DOWN:
            src, dst = fsd.at[c], fu.at[k, c]
        elif d == RIGHT:
            src, dst = vf.at[c, pl.ds(8 * (angs - 1), 8)], fl.at[k, c]
        else:
            src, dst = vf.at[c, pl.ds(0, 8)], fr.at[k, c]
        return pltpu.make_async_remote_copy(
            src_ref=src, dst_ref=dst, send_sem=fsend.at[k, g, d], recv_sem=frecv.at[k, g, d],
            device_id=device(*SHIFT[d]), device_id_type=MESH)

    def fine_start(k, g):
        for d in range(4):
            guarded(SHIFT[d][1], lambda d=d: fine(k, g, d).start())

    def fine_wait(k, g):
        for d in range(4):
            guarded(SHIFT[d][1], lambda d=d: fine(k, g, d).wait_send())
            guarded(-SHIFT[d][1], lambda d=d: fine(k, g, d).wait_recv())

    def corner_tiles(k, c):
        low = [co[k, c, 3 + h, pl.ds(0, 8), :] for h in range(4)]
        high = [co[k, c, 3 + h, pl.ds(8, 8), :] for h in range(4)]
        for t in range(2):
            sr[c, pl.ds(8 * t, 8), :] = jnp.where(sub < 4, roll(high[2 * t], 4), high[2 * t + 1])
            sl[c, pl.ds(8 * t, 8), :] = jnp.where(sub < 4, low[2 * t], roll(low[2 * t + 1], 4))
        return (
            jnp.where(sub == 5, roll(high[2], -2), high[3]),
            jnp.where(sub == 2, roll(low[2], 2), low[3]),
            jnp.where(sub == 5, roll(high[1], -2), high[0]),
            jnp.where(sub == 2, roll(low[1], 2), low[0]),
        )

    def merge(d, even, odd):
        if d in (RU, RD):
            return jnp.where(sub < 4, roll(even, 4), odd)
        return jnp.where(sub < 4, even, roll(odd, 4))

    def pack_pair(k, pair):
        even, odd = corner_tiles(k, 2 * pair), corner_tiles(k, 2 * pair + 1)
        for d in (RU, LU, RD, LD):
            sc[d - 4, pair] = merge(d, even[d - 4], odd[d - 4])

    def halo(k, c, pair, parity, h):
        if 0 <= h < 4:
            t = h // 2
            q, p = hr[k, c, pl.ds(8 * t, 8), :], hl[k, c, pl.ds(8 * t, 8), :]
            if h % 2 == 0:
                return jnp.where(sub < 4, q, roll(p, 4))
            return jnp.where(sub < 4, roll(q, 4), p)
        left = rc[k, (RU if h < 0 else RD) - 4, pair]
        right = rc[k, (LU if h < 0 else LD) - 4, pair]
        if parity == 0:
            left = roll(left, 4)
        else:
            right = roll(right, 4)
        if h in (-2, 5):
            left, right = roll(left, 2), roll(right, -2)
        return jnp.where(sub < 4, right, left)

    def ring_row(k, c, pair, parity, h):
        return [co[k, c, 3 + h, pl.ds(0, 8), :], co[k, c, 3 + h, pl.ds(8, 8), :], halo(k, c, pair, parity, h)]

    for copy in in_copies:
        copy.wait()

    def weigh(a, carry):
        rows = pl.ds(pl.multiple_of(a * 8, 8), 8)
        kind = mat[rows, :]
        stiff = zero
        for level in range(modulus.shape[0]):
            stiff = stiff + jnp.where(kind == level, modulus[level], 0.0)
        w = jnp.sqrt(stiff)
        s = sup[rows, :].astype(F32)
        d = SIGMA * w * w + SPRING * s
        weight[rows, :] = w
        spring[rows, :] = s
        diag[rows, :] = d
        kf[rows, :] = OMEGA / d
        return carry

    lax.fori_loop(0, angs, weigh, 0, unroll=4)
    for j in range(4):
        for b in range(2):
            wc = 0.25 * quad(weight, j, b)
            s = 0.25 * quad(spring, j, b)
            kd = OMEGA / (SIGMA * wc * wc + SPRING * s)
            kv[j, pl.ds(8 * b, 8), :] = 0.5 * wc * kd
            iw[j, pl.ds(8 * b, 8), :] = 0.5 / wc
            co[0, pcol, 3 + j, pl.ds(8 * b, 8), :] = wc * wc * kd
    tiles = corner_tiles(0, pcol)
    for d in (RU, LU, RD, LD):
        sc[d - 4, pcol // 2] = merge(d, tiles[d - 4], zero)

    diagonals = 2 * (has_up.astype(jnp.int32) + has_down.astype(jnp.int32))
    pl.semaphore_wait(barrier, na - 1 + nh - 1 + diagonals)
    deep_start(0, groups, pcol, 1)

    def add_moment(g, c, m, acc):
        total = jnp.sum(jnp.sum(acc, axis=0, keepdims=True), axis=1, keepdims=True)
        tsum[g] += jnp.where(jnp.logical_and(sub == m, lane == c), total, 0.0)

    def restrict(k, c):
        for j in range(4):
            for b in range(2):
                co[k, c, 3 + j, pl.ds(8 * b, 8), :] = kv[j, pl.ds(8 * b, 8), :] * quad(res, j, b, k, c)

    def send_deep(k, g):
        lax.fori_loop(0, per // 2, lambda i, carry: (pack_pair(k, g * (per // 2) + i), carry)[1], 0)
        deep_start(k, g, g * per, per)

    total_angles = na * angs

    def first(g, carry):
        load_copy(g).wait()
        tsum[g] = zero

        def column(i, carry):
            c = g * per + i
            amount = jnp.where(lax.rem(c, 3) == 2, -LOAD, 0.0)
            spot = jnp.full(T, me_a * angs, jnp.int32) - positions[c // 3]
            for a in range(angs):
                apart = jnp.abs(spot + a)
                near = jnp.minimum(apart, total_angles - apart) < angs
                res[0, c, pl.ds(8 * a, 8), :] += jnp.where(near, amount, 0.0)
            restrict(0, c)
            return carry

        lax.fori_loop(0, per, column, 0)
        send_deep(0, g)
        return carry

    lax.fori_loop(0, groups, first, 0)

    deep_wait(0, groups, pcol, 1)
    for h in range(-2, 6):
        row = ring_row(0, pcol, pcol // 2, 0, h)
        for b in range(3):
            pr[h + 2, b] = row[b]

    def sweeps(k, c, pair, parity):
        v0 = {h: ring_row(k, c, pair, parity, h) for h in range(-2, 6)}
        for h in range(-2, 6):
            for b in range(3):
                ring[0, parity, h + 2, b] = v0[h][b]
        outer = {h: [co[k, c, 3 + h, pl.ds(0, 8), :], co[k, c, 3 + h, pl.ds(8, 8), :]] for h in (-3, 6)}
        for sweep in range(3):
            def get(h, b):
                if h in outer:
                    return outer[h][b]
                return ring[sweep, parity, h + 2, b]

            for h in range(-2 + sweep, 6 - sweep):
                edge = h in (-2 + sweep, 5 - sweep)
                me = [get(h, b) for b in range(3)]
                back = [roll(x, 1) for x in me]
                ahead = [roll(x, -1) for x in me]
                for b in range(2 if edge or sweep == 2 else 3):
                    beside = jnp.where(sub == 0, back[b - 1], back[b]) + jnp.where(sub == 7, ahead[(b + 1) % 3], ahead[b])
                    beside = beside + (get(h - 1, b) + get(h + 1, b)) + lanes(me[b])
                    new = (1.0 - OMEGA) * me[b] + ring[0, parity, h + 2, b] + pr[h + 2, b] * beside
                    if sweep < 2:
                        ring[sweep + 1, parity, h + 2, b] = new
                    else:
                        new = new * iw[h, pl.ds(8 * b, 8), :]
                        for da in range(2):
                            for dh in range(2):
                                pe[parity, pl.ds(b * 128 + da * 8 + 2 * h + dh, 8, stride=16), :] = new

    def prolong(k, g, c, parity):
        acc = zero
        for a in range(angs):
            rows = pl.ds(8 * a, 8)
            r = res[k, c, rows, :]
            z = kf[rows, :] * r + pe[parity, rows, :]
            ys[k, c, rows, :] = z
            acc = acc + r * z
            vf[c, rows, :] = weight[rows, :] * z
        add_moment(g, c, 2 * k, acc)
        for i in range(4):
            fsu[c, pl.ds(8 * i, 8), :] = vf[c, pl.ds(64 * i + 7, 8, stride=8), :]
            fsd[c, pl.ds(8 * i, 8), :] = vf[c, pl.ds(64 * i, 8, stride=8), :]

    def precondition(k, g):
        deep_wait(k, g, g * per, per)

        def pair_body(i, carry):
            pair = g * (per // 2) + i
            for parity in range(2):
                sweeps(k, 2 * pair + parity, pair, parity)
            for parity in range(2):
                prolong(k, g, 2 * pair + parity, parity)
            return carry

        lax.fori_loop(0, per // 2, pair_body, 0)
        fine_start(k, g)

    def apply_fine(k, g):
        fine_wait(k, g)

        def column(i, carry):
            c = g * per + i
            acc = zero
            before, now = fl[k, c], vf[c, pl.ds(0, 8), :]
            for a in range(angs):
                rows = pl.ds(8 * a, 8)
                after = vf[c, pl.ds(8 * (a + 1), 8), :] if a < angs - 1 else fr[k, c]
                below = jnp.where(sub == 0, fd[k, c, pl.ds(a, 1), :], roll(now, 1))
                above = jnp.where(sub == 7, fu[k, c, pl.ds(a, 1), :], roll(now, -1))
                beside = (before + after) + (below + above) + lanes(now)
                z = ys[k, c, rows, :]
                r = diag[rows, :] * z - weight[rows, :] * beside - res[k, c, rows, :]
                res[k + 1, c, rows, :] = r
                acc = acc + r * z
                before, now = now, after
            add_moment(g, c, 2 * k + 1, acc)
            if k + 1 < STEPS:
                restrict(k + 1, c)
            return carry

        lax.fori_loop(0, per, column, 0)
        if k + 1 < STEPS:
            send_deep(k + 1, g)

    def psum_start(g, stage):
        n, me, slots = (na, me_a, pa) if stage == 0 else (nh, me_h, pb)

        def one(d, carry):
            other = lax.rem(me + d, n)
            where = {"ang": other, "hgt": me_h} if stage == 0 else {"ang": me_a, "hgt": other}
            pltpu.make_async_remote_copy(
                src_ref=tsum.at[g + stage * groups], dst_ref=slots.at[g, me],
                send_sem=psend.at[stage, g], recv_sem=precv.at[stage, g],
                device_id=where, device_id_type=MESH).start()
            return carry

        lax.fori_loop(1, n, one, 0)

    def psum_wait(g, stage):
        n, me, slots = (na, me_a, pa) if stage == 0 else (nh, me_h, pb)
        many = slots.at[g, pl.ds(0, n - 1)]
        pltpu.make_async_copy(many, many, psend.at[stage, g]).wait()
        pltpu.make_async_copy(many, many, precv.at[stage, g]).wait()
        slots[g, me] = tsum[g + stage * groups]
        total = slots[g, 0]
        for i in range(1, n):
            total = total + slots[g, i]
        return total

    for k in range(STEPS):
        lax.fori_loop(0, groups, lambda g, carry: (precondition(k, g), carry)[1], 0)
        if k + 1 < STEPS:
            lax.fori_loop(0, groups, lambda g, carry: (apply_fine(k, g), carry)[1], 0)

    def last(g, carry):
        apply_fine(STEPS - 1, g)
        psum_start(g, 0)
        return carry

    lax.fori_loop(0, groups, last, 0)

    def middle(g, carry):
        tsum[g + groups] = psum_wait(g, 0)
        psum_start(g, 1)
        return carry

    lax.fori_loop(0, groups, middle, 0)

    def out_copies(g):
        c = pl.ds(g * per, per)
        return (pltpu.make_async_copy(ys.at[0, c], out_x.at[c], out_sem.at[0, g]),
                pltpu.make_async_copy(res.at[0, c], out_r.at[c], out_sem.at[1, g]))

    def finish(g, carry):
        total = psum_wait(g, 1)
        m = [total[i:i + 1, :] for i in range(2 * STEPS)]
        none = jnp.zeros_like(m[0])
        one = jnp.ones_like(m[0])
        way, left, made = [one, none, none], [one, none, none, none], [none] * 3
        rz = m[0]
        for k in range(STEPS):
            image = [none] * 4
            for j in range(k + 1):
                image[j + 1] = image[j + 1] + way[j]
                image[j] = image[j] + way[j]
            curve = none
            for i in range(k + 1):
                for j in range(k + 2):
                    curve = curve + way[i] * image[j] * m[i + j]
            alpha = rz / curve
            made = [made[j] + alpha * way[j] for j in range(3)]
            left = [left[j] - alpha * image[j] for j in range(4)]
            if k + 1 < STEPS:
                new = none
                for i in range(k + 2):
                    for j in range(k + 2):
                        new = new + left[i] * left[j] * m[i + j]
                beta = new / rz
                way = [left[j] + beta * way[j] for j in range(3)]
                rz = new

        def column(i, carry):
            c = g * per + i

            def pick(x):
                return jnp.sum(jnp.where(lane[0:1] == c, x, 0.0), axis=1, keepdims=True)

            x_of = [jnp.broadcast_to(pick(x), T) for x in made]
            r_of = [jnp.broadcast_to(pick(x), T) for x in left]
            for a in range(angs):
                rows = pl.ds(8 * a, 8)
                x = x_of[0] * ys[0, c, rows, :] + x_of[1] * ys[1, c, rows, :] + x_of[2] * ys[2, c, rows, :]
                r = (r_of[0] * res[0, c, rows, :] + r_of[1] * res[1, c, rows, :]
                     + r_of[2] * res[2, c, rows, :] + r_of[3] * res[3, c, rows, :])
                ys[0, c, rows, :] = x
                res[0, c, rows, :] = r
            return carry

        lax.fori_loop(0, per, column, 0)
        for copy in out_copies(g):
            copy.start()
        return carry

    lax.fori_loop(0, groups, finish, 0)
    for g in range(groups):
        for copy in out_copies(g):
            copy.wait()


def body(loads, material, support, modulus, positions):
    cases, comps, angs, rows, radial = loads.shape
    cols = cases * comps
    na, nh = lax.axis_size("ang"), lax.axis_size("hgt")
    flat = angs * rows
    any_spec = pl.BlockSpec(memory_space=pl.ANY)
    smem = pl.BlockSpec(memory_space=pltpu.SMEM)
    out = jax.ShapeDtypeStruct((cols, flat, radial), F32)
    v = lambda *shape: pltpu.VMEM((*shape, 128), F32)
    dma = lambda *shape: pltpu.SemaphoreType.DMA(shape)
    x, r = pl.pallas_call(
        kernel,
        out_shape=(out, out),
        in_specs=[smem, smem, any_spec, any_spec, any_spec],
        out_specs=(any_spec, any_spec),
        scratch_shapes=[
            pltpu.VMEM((flat, 128), jnp.int32), pltpu.VMEM((flat, 128), jnp.int32),
            v(flat), v(flat), v(flat), v(flat), v(4, 16), v(4, 16),
            v(STEPS + 1, cols, flat), v(STEPS, cols, flat), v(cols, flat), v(2, flat),
            v(STEPS, cols + 1, 10, 16),
            v(cols + 1, 16), v(cols + 1, 16), v(4, cols // 2 + 1, 8),
            v(STEPS, cols + 1, 16), v(STEPS, cols + 1, 16), v(STEPS, 4, cols // 2 + 1, 8),
            v(8, 3, 8), v(3, 2, 8, 3, 8),
            v(cols, 32), v(cols, 32), v(STEPS, cols, 32), v(STEPS, cols, 32),
            v(STEPS, cols, 8), v(STEPS, cols, 8),
            v(2 * GROUPS, 8), v(GROUPS, na, 8), v(GROUPS, nh, 8),
            dma(GROUPS + 2), dma(STEPS, GROUPS + 1, 8), dma(STEPS, GROUPS + 1, 8),
            dma(STEPS, GROUPS, 4), dma(STEPS, GROUPS, 4), dma(2, GROUPS), dma(2, GROUPS), dma(2, GROUPS),
        ],
        compiler_params=pltpu.CompilerParams(
            collective_id=0, has_side_effects=True, vmem_limit_bytes=60 * 1024 * 1024),
        name="girder_cg",
    )(modulus, positions, loads.reshape(cols, flat, radial), material.reshape(flat, radial), support.reshape(flat, radial))
    return x.reshape(loads.shape), r.reshape(loads.shape)


def solution(mesh):
    field = P(None, None, "ang", "hgt", None)
    cell = P("ang", "hgt", None)
    return jax.shard_map(body, mesh=mesh, in_specs=(field, cell, cell, P(), P()),
                         out_specs=(field, field), check_vma=False)
```

time: 556 us -> 72.2 us (0.13); the launches traced: 548 us -> 72 us
  blocking collectives: 356 us -> 0 us
  starting transfers between devices: 124 us -> 0 us
  Pallas kernels: 0 us -> 67.5 us
  other arithmetic: 35.7 us -> 0 us
  waiting for transfers between devices: 20.6 us -> 0 us
  local copies, waits for them, and re-layouts: 10.2 us -> 3.92 us
    psum x5 -> x0, blocking collectives: 356 us -> none  [the longest x3 218 us: projection(): lax.psum(jnp.sum(a * b, axis=(2, 3, 4)), ('ang', 'hgt'))]
    ppermute x48 -> x0, starting transfers between devices: 124 us -> none  [the longest x24 67.4 us: padded_2(): lax.ppermute(lax.slice_in_dim(block, 0, width, axis=dim), axis, backward)]
    pallas_call x0 -> x1, Pallas kernels: none -> 67.5 us  [body(): pl.pallas_call(kernel, out_shape=(out, out), in_specs=[smem, smem, any_sp...]
    ppermute x48 -> x0, waiting for transfers between devices: 20.6 us -> none  [the longest x24 13.5 us: padded_2(): lax.ppermute(lax.slice_in_dim(block, 0, width, axis=dim), axis, backward)]
    reduce_sum x11 -> x0, other arithmetic: 14.2 us -> none  [the longest x3 8.4 us: body(): curve = lax.psum(jnp.sum(direction * image, axis=(2, 3, 4)), ('ang', 'hgt'))]
    mul x17 -> x0, other arithmetic: 10.9 us -> none  [the longest x3 5.06 us: fine_apply(): v = weight * u]
    sub x3 -> x0, other arithmetic: 7.12 us -> none  [body(): residual = residual - alpha * image]
  transfers between devices with their start and end apart: 48 -> 0, of which waited for: 24 -> 0; matrix products, arithmetic and copies ran while one was open for 0% -> 0% of each run, Pallas kernels for 0% -> 0%
where the time goes in v1:
time: 72.2 us; the launch traced here: 72 us
  Pallas kernels  67.5 us (93%)
  local copies, waits for them, and re-layouts  3.92 us (5%)
    pallas_call x1, Pallas kernels, body(): pl.pallas_call(kernel, out_shape=(out, out), in_specs=[smem, smem, any_sp...  67.5 us
    unnamed x4, local copies, waits for them, and re-layouts  3.92 us

profile of v1, /device:TPU:1, one launch (start us, length us, event | category | flops | bytes accessed | tf_op | source)
XLA Modules:
  0.0 72.0 jit_solution(11145350407504858281)
XLA Ops:
  0.6 67.5 %girder_cg.1 = (f32[12,256,128]{2,1,0:T(8,128)}, f32[12,256,128]{2,1,0:T(8,128)}) custom-call(f32[8]{0:T(128)} %modulus.1, s32[4]{0:T(128)} %positions.1, f32[12,256,128]{2,1,0:T(8,128)} %bitcast.5, s32[256,128]{1,0:T(8,128)} %bitcast.8, s32[256,128]{1,0:T(8,128)} %bitcast.9), custom_call_target="tpu_custom_call" | custom-call | tf_op jit(solution)/shard_map/girder_cg/pallas_call | solution.py:494
  68.1 0.0 copy-start
  68.1 2.8 %copy.9 = f32[4,3,32,8,128]{4,3,2,1,0:T(8,128)} copy(f32[4,3,32,8,128]{4,3,2,1,0:T(8,128)} %bitcast.7) | data formatting | bytes 3145728
  70.9 0.0 copy-done
  70.9 1.1 %copy.10 = f32[4,3,32,8,128]{4,3,2,1,0:T(8,128)} copy(f32[4,3,32,8,128]{4,3,2,1,0:T(8,128)S(1)} %bitcast.6) | data formatting | bytes 3145728
Async XLA Ops:
  68.1 2.8 %copy-start = (f32[12,256,128]{2,1,0:T(8,128)S(1)}, f32[12,256,128]{2,1,0:T(8,128)}, u32[]{:S(2)}) copy-start(f32[12,256,128]{2,1,0:T(8,128)} %get-tuple-element.5) | copy-start | bytes 4718596

commit v2 on v1

--- a/solution.py
+++ b/solution.py
@@ -12,7 +12,7 @@
 SPRING = 20.0
 OMEGA = 0.8
 LOAD = 3.0
-GROUPS = 3
+GROUPS = 6
 MESH = pl.DeviceIdType.MESH
 F32 = jnp.float32
 T = (8, 128)
@@ -22,11 +22,11 @@
 
 def kernel(
     modulus, positions, loads, material, support,
-    out_x, out_r,
+    res, ys, sums,
     mat, sup, weight, spring, diag, kf, kv, iw,
-    res, ys, vf, pe, co, sr, sl, sc, hl, hr, rc, pr, ring,
-    fsu, fsd, fu, fd, fl, fr, tsum, pa, pb,
-    in_sem, dsend, drecv, fsend, frecv, psend, precv, out_sem,
+    vf, pe, co, sr, sl, sc, hl, hr, rc, pr, ring,
+    fsu, fsd, fu, fd, fl, fr, moments, tsum, pa, pb,
+    in_sem, dsend, drecv, fsend, frecv, psend, precv,
 ):
     na, nh = lax.axis_size("ang"), lax.axis_size("hgt")
     me_a, me_h = lax.axis_index("ang"), lax.axis_index("hgt")
@@ -119,9 +119,6 @@
             return carry
 
         lax.fori_loop(0, cols // 2 + 1, three, 0)
-
-    pl.when(jnp.logical_not(has_down))(lambda: clear(0, (RU - 4, LU - 4), fd))
-    pl.when(jnp.logical_not(has_up))(lambda: clear(7, (RD - 4, LD - 4), fu))
 
     def deep(k, slot, first, count, d):
         c = pl.ds(first, count)
@@ -250,10 +247,6 @@
     pl.semaphore_wait(barrier, na - 1 + nh - 1 + diagonals)
     deep_start(0, groups, pcol, 1)
 
-    def add_moment(g, c, m, acc):
-        total = jnp.sum(jnp.sum(acc, axis=0, keepdims=True), axis=1, keepdims=True)
-        tsum[g] += jnp.where(jnp.logical_and(sub == m, lane == c), total, 0.0)
-
     def restrict(k, c):
         for j in range(4):
             for b in range(2):
@@ -265,9 +258,8 @@
 
     total_angles = na * angs
 
-    def first(g, carry):
+    def first(g):
         load_copy(g).wait()
-        tsum[g] = zero
 
         def column(i, carry):
             c = g * per + i
@@ -282,15 +274,13 @@
 
         lax.fori_loop(0, per, column, 0)
         send_deep(0, g)
-        return carry
-
-    lax.fori_loop(0, groups, first, 0)
-
-    deep_wait(0, groups, pcol, 1)
-    for h in range(-2, 6):
-        row = ring_row(0, pcol, pcol // 2, 0, h)
-        for b in range(3):
-            pr[h + 2, b] = row[b]
+
+    def coarse_ring():
+        deep_wait(0, groups, pcol, 1)
+        for h in range(-2, 6):
+            row = ring_row(0, pcol, pcol // 2, 0, h)
+            for b in range(3):
+                pr[h + 2, b] = row[b]
 
     def sweeps(k, c, pair, parity):
         v0 = {h: ring_row(k, c, pair, parity, h) for h in range(-2, 6)}
@@ -330,7 +320,7 @@
             ys[k, c, rows, :] = z
             acc = acc + r * z
             vf[c, rows, :] = weight[rows, :] * z
-        add_moment(g, c, 2 * k, acc)
+        moments[c, 2 * k] = acc
         for i in range(4):
             fsu[c, pl.ds(8 * i, 8), :] = vf[c, pl.ds(64 * i + 7, 8, stride=8), :]
             fsd[c, pl.ds(8 * i, 8), :] = vf[c, pl.ds(64 * i, 8, stride=8), :]
@@ -367,7 +357,7 @@
                 res[k + 1, c, rows, :] = r
                 acc = acc + r * z
                 before, now = now, after
-            add_moment(g, c, 2 * k + 1, acc)
+            moments[c, 2 * k + 1] = acc
             if k + 1 < STEPS:
                 restrict(k + 1, c)
             return carry
@@ -376,109 +366,105 @@
         if k + 1 < STEPS:
             send_deep(k + 1, g)
 
-    def psum_start(g, stage):
+    def reduce_moments(g):
+        for i in range(per):
+            c = g * per + i
+            rows = zero
+            for m in range(2 * STEPS):
+                rows = jnp.where(sub == m, jnp.sum(moments[c, m], axis=0, keepdims=True), rows)
+            tsum[0] += jnp.where(lane == c, jnp.sum(rows, axis=1, keepdims=True), 0.0)
+
+    def psum(stage):
         n, me, slots = (na, me_a, pa) if stage == 0 else (nh, me_h, pb)
 
         def one(d, carry):
             other = lax.rem(me + d, n)
             where = {"ang": other, "hgt": me_h} if stage == 0 else {"ang": me_a, "hgt": other}
             pltpu.make_async_remote_copy(
-                src_ref=tsum.at[g + stage * groups], dst_ref=slots.at[g, me],
-                send_sem=psend.at[stage, g], recv_sem=precv.at[stage, g],
+                src_ref=tsum.at[stage], dst_ref=slots.at[me], send_sem=psend.at[stage], recv_sem=precv.at[stage],
                 device_id=where, device_id_type=MESH).start()
             return carry
 
         lax.fori_loop(1, n, one, 0)
-
-    def psum_wait(g, stage):
-        n, me, slots = (na, me_a, pa) if stage == 0 else (nh, me_h, pb)
-        many = slots.at[g, pl.ds(0, n - 1)]
-        pltpu.make_async_copy(many, many, psend.at[stage, g]).wait()
-        pltpu.make_async_copy(many, many, precv.at[stage, g]).wait()
-        slots[g, me] = tsum[g + stage * groups]
-        total = slots[g, 0]
+        slots[me] = tsum[stage]
+        many = slots.at[pl.ds(0, n - 1)]
+        pltpu.make_async_copy(many, many, psend.at[stage]).wait()
+        pltpu.make_async_copy(many, many, precv.at[stage]).wait()
+        total = slots[0]
         for i in range(1, n):
-            total = total + slots[g, i]
+            total = total + slots[i]
         return total
 
+    def stage(s, g):
+        if s == 0:
+            first(g)
+        elif s % 2:
+            precondition(s // 2, g)
+        else:
+            apply_fine(s // 2 - 1, g)
+            if s == 2 * STEPS:
+                reduce_moments(g)
+
+    tsum[0] = zero
+    for t in range(2 * STEPS + 2):
+        if t == 1:
+            pl.when(jnp.logical_not(has_down))(lambda: clear(0, (RU - 4, LU - 4), fd))
+            pl.when(jnp.logical_not(has_up))(lambda: clear(7, (RD - 4, LD - 4), fu))
+            coarse_ring()
+
+        def both(i, carry):
+            if t <= 2 * STEPS:
+                stage(t, 2 * i)
+            if t >= 1:
+                stage(t - 1, 2 * i + 1)
+            return carry
+
+        lax.fori_loop(0, groups // 2, both, 0)
+
+    tsum[1] = psum(0)
+    sums[...] = psum(1)
+
+
+def combine(sums, res, ys, out_x, out_r):
+    m = [sums[i:i + 1, :] for i in range(2 * STEPS)]
+    none = jnp.zeros_like(m[0])
+    one = jnp.ones_like(m[0])
+    way, left, made = [one, none, none], [one, none, none, none], [none] * 3
+    rz = m[0]
     for k in range(STEPS):
-        lax.fori_loop(0, groups, lambda g, carry: (precondition(k, g), carry)[1], 0)
+        image = [none] * 4
+        for j in range(k + 1):
+            image[j + 1] = image[j + 1] + way[j]
+            image[j] = image[j] + way[j]
+        curve = none
+        for i in range(k + 1):
+            for j in range(k + 2):
+                curve = curve + way[i] * image[j] * m[i + j]
+        alpha = rz / curve
+        made = [made[j] + alpha * way[j] for j in range(3)]
+        left = [left[j] - alpha * image[j] for j in range(4)]
         if k + 1 < STEPS:
-            lax.fori_loop(0, groups, lambda g, carry: (apply_fine(k, g), carry)[1], 0)
-
-    def last(g, carry):
-        apply_fine(STEPS - 1, g)
-        psum_start(g, 0)
-        return carry
-
-    lax.fori_loop(0, groups, last, 0)
-
-    def middle(g, carry):
-        tsum[g + groups] = psum_wait(g, 0)
-        psum_start(g, 1)
-        return carry
-
-    lax.fori_loop(0, groups, middle, 0)
-
-    def out_copies(g):
-        c = pl.ds(g * per, per)
-        return (pltpu.make_async_copy(ys.at[0, c], out_x.at[c], out_sem.at[0, g]),
-                pltpu.make_async_copy(res.at[0, c], out_r.at[c], out_sem.at[1, g]))
-
-    def finish(g, carry):
-        total = psum_wait(g, 1)
-        m = [total[i:i + 1, :] for i in range(2 * STEPS)]
-        none = jnp.zeros_like(m[0])
-        one = jnp.ones_like(m[0])
-        way, left, made = [one, none, none], [one, none, none, none], [none] * 3
-        rz = m[0]
-        for k in range(STEPS):
-            image = [none] * 4
-            for j in range(k + 1):
-                image[j + 1] = image[j + 1] + way[j]
-                image[j] = image[j] + way[j]
-            curve = none
-            for i in range(k + 1):
+            new = none
+            for i in range(k + 2):
                 for j in range(k + 2):
-                    curve = curve + way[i] * image[j] * m[i + j]
-            alpha = rz / curve
-            made = [made[j] + alpha * way[j] for j in range(3)]
-            left = [left[j] - alpha * image[j] for j in range(4)]
-            if k + 1 < STEPS:
-                new = none
-                for i in range(k + 2):
-                    for j in range(k + 2):
-                        new = new + left[i] * left[j] * m[i + j]
-                beta = new / rz
-                way = [left[j] + beta * way[j] for j in range(3)]
-                rz = new
-
-        def column(i, carry):
-            c = g * per + i
-
-            def pick(x):
-                return jnp.sum(jnp.where(lane[0:1] == c, x, 0.0), axis=1, keepdims=True)
-
-            x_of = [jnp.broadcast_to(pick(x), T) for x in made]
-            r_of = [jnp.broadcast_to(pick(x), T) for x in left]
-            for a in range(angs):
-                rows = pl.ds(8 * a, 8)
-                x = x_of[0] * ys[0, c, rows, :] + x_of[1] * ys[1, c, rows, :] + x_of[2] * ys[2, c, rows, :]
-                r = (r_of[0] * res[0, c, rows, :] + r_of[1] * res[1, c, rows, :]
-                     + r_of[2] * res[2, c, rows, :] + r_of[3] * res[3, c, rows, :])
-                ys[0, c, rows, :] = x
-                res[0, c, rows, :] = r
-            return carry
-
-        lax.fori_loop(0, per, column, 0)
-        for copy in out_copies(g):
-            copy.start()
-        return carry
-
-    lax.fori_loop(0, groups, finish, 0)
-    for g in range(groups):
-        for copy in out_copies(g):
-            copy.wait()
+                    new = new + left[i] * left[j] * m[i + j]
+            beta = new / rz
+            way = [left[j] + beta * way[j] for j in range(3)]
+            rz = new
+
+    c = pl.program_id(0)
+    lane = lax.broadcasted_iota(jnp.int32, (1, 128), 1)
+
+    def pick(x):
+        return jnp.broadcast_to(jnp.sum(jnp.where(lane == c, x, 0.0), axis=1, keepdims=True), T)
+
+    x_of = [pick(x) for x in made]
+    r_of = [pick(x) for x in left]
+    for a in range(out_x.shape[1] // 8):
+        rows = pl.ds(8 * a, 8)
+        out_x[0, rows, :] = x_of[0] * ys[0, c, rows, :] + x_of[1] * ys[1, c, rows, :] + x_of[2] * ys[2, c, rows, :]
+        out_r[0, rows, :] = (r_of[0] * res[0, c, rows, :] + r_of[1] * res[1, c, rows, :]
+                             + r_of[2] * res[2, c, rows, :] + r_of[3] * res[3, c, rows, :])
 
 
 def body(loads, material, support, modulus, positions):
@@ -486,34 +472,45 @@
     cols = cases * comps
     na, nh = lax.axis_size("ang"), lax.axis_size("hgt")
     flat = angs * rows
-    any_spec = pl.BlockSpec(memory_space=pl.ANY)
+    any_spec = pl.BlockSpec(memory_space=pltpu.HBM)
     smem = pl.BlockSpec(memory_space=pltpu.SMEM)
-    out = jax.ShapeDtypeStruct((cols, flat, radial), F32)
+    vmem = pl.BlockSpec(memory_space=pltpu.VMEM)
     v = lambda *shape: pltpu.VMEM((*shape, 128), F32)
     dma = lambda *shape: pltpu.SemaphoreType.DMA(shape)
-    x, r = pl.pallas_call(
+    res, ys, sums = pl.pallas_call(
         kernel,
-        out_shape=(out, out),
+        out_shape=(v(STEPS + 1, cols, flat), v(STEPS, cols, flat), v(8)),
         in_specs=[smem, smem, any_spec, any_spec, any_spec],
-        out_specs=(any_spec, any_spec),
+        out_specs=(vmem, vmem, vmem),
         scratch_shapes=[
             pltpu.VMEM((flat, 128), jnp.int32), pltpu.VMEM((flat, 128), jnp.int32),
             v(flat), v(flat), v(flat), v(flat), v(4, 16), v(4, 16),
-            v(STEPS + 1, cols, flat), v(STEPS, cols, flat), v(cols, flat), v(2, flat),
+            v(cols, flat), v(2, flat),
             v(STEPS, cols + 1, 10, 16),
             v(cols + 1, 16), v(cols + 1, 16), v(4, cols // 2 + 1, 8),
             v(STEPS, cols + 1, 16), v(STEPS, cols + 1, 16), v(STEPS, 4, cols // 2 + 1, 8),
             v(8, 3, 8), v(3, 2, 8, 3, 8),
             v(cols, 32), v(cols, 32), v(STEPS, cols, 32), v(STEPS, cols, 32),
             v(STEPS, cols, 8), v(STEPS, cols, 8),
-            v(2 * GROUPS, 8), v(GROUPS, na, 8), v(GROUPS, nh, 8),
+            v(cols, 2 * STEPS, 8), v(2, 8), v(na, 8), v(nh, 8),
             dma(GROUPS + 2), dma(STEPS, GROUPS + 1, 8), dma(STEPS, GROUPS + 1, 8),
-            dma(STEPS, GROUPS, 4), dma(STEPS, GROUPS, 4), dma(2, GROUPS), dma(2, GROUPS), dma(2, GROUPS),
+            dma(STEPS, GROUPS, 4), dma(STEPS, GROUPS, 4), dma(2), dma(2),
         ],
         compiler_params=pltpu.CompilerParams(
-            collective_id=0, has_side_effects=True, vmem_limit_bytes=60 * 1024 * 1024),
+            collective_id=0, has_side_effects=True, vmem_limit_bytes=55 * 1000 * 1000),
         name="girder_cg",
     )(modulus, positions, loads.reshape(cols, flat, radial), material.reshape(flat, radial), support.reshape(flat, radial))
+    out = jax.ShapeDtypeStruct((cols, flat, radial), F32)
+    block = pl.BlockSpec((1, flat, radial), lambda c: (c, 0, 0))
+    x, r = pl.pallas_call(
+        combine,
+        grid=(cols,),
+        out_shape=(out, out),
+        in_specs=[vmem, vmem, vmem],
+        out_specs=(block, block),
+        compiler_params=pltpu.CompilerParams(vmem_limit_bytes=16 * 1024 * 1024),
+        name="girder_combine",
+    )(sums, res, ys)
     return x.reshape(loads.shape), r.reshape(loads.shape)
 
 

time: 72.2 us -> 73.9 us (1.024)
  Pallas kernels: 67.5 us -> 73.1 us
  local copies, waits for them, and re-layouts: 3.92 us -> 0 us
    pallas_call x1 -> x2, Pallas kernels: 67.5 us -> 73.1 us  [the longest x1 67.6 us: body(): pl.pallas_call(kernel, out_shape=(v(STEPS + 1, cols, flat), v(STEPS, cols...]
    unnamed x4 -> x0, local copies, waits for them, and re-layouts: 3.92 us -> none
where the time goes in v2:
time: 73.9 us; the launch traced here: 73.7 us
  Pallas kernels  73.1 us (99%)
    pallas_call x1, Pallas kernels, body(): pl.pallas_call(kernel, out_shape=(v(STEPS + 1, cols, flat), v(STEPS, cols...  67.6 us
    pallas_call x1, Pallas kernels, body(): pl.pallas_call(combine, grid=(cols,), out_shape=(out, out), in_specs=[vme...  5.46 us

profile of v2, /device:TPU:1, one launch (start us, length us, event | category | flops | bytes accessed | tf_op | source)
XLA Modules:
  0.0 73.7 jit_solution(4265214921867021144)
XLA Ops:
  0.6 67.6 %girder_cg.1 = (f32[4,12,256,128]{3,2,1,0:T(8,128)S(1)}, f32[3,12,256,128]{3,2,1,0:T(8,128)S(1)}, f32[8,128]{1,0:T(8,128)S(1)}) custom-call(f32[8]{0:T(128)} %modulus.1, s32[4]{0:T(128)} %positions.1, f32[12,256,128]{2,1,0:T(8,128)} %bitcast.5, s32[256,128]{1,0:T(8,128)} %bitcast.6, s32[256,128]{1,0:T(8,128)} %bitcast.7), custom_call_target="tpu_custom_call" | custom-call | tf_op jit(solution)/shard_map/girder_cg/pallas_call | solution.py:480
  68.3 5.5 %girder_combine.1 = (f32[12,256,128]{2,1,0:T(8,128)}, f32[12,256,128]{2,1,0:T(8,128)}) custom-call(f32[8,128]{1,0:T(8,128)S(1)} %get-tuple-element.7.sums, f32[4,12,256,128]{3,2,1,0:T(8,128)S(1)} %get-tuple-element.8.res, f32[3,12,256,128]{3,2,1,0:T(8,128)S(1)} %get-tuple-element.9.ys), custom_call_target="tpu_custom_call" | custom-call | tf_op jit(solution)/shard_map/girder_combine/pallas_call | solution.py:505

commit v3 on v2

--- a/solution.py
+++ b/solution.py
@@ -12,7 +12,7 @@
 SPRING = 20.0
 OMEGA = 0.8
 LOAD = 3.0
-GROUPS = 6
+GROUPS = 3
 MESH = pl.DeviceIdType.MESH
 F32 = jnp.float32
 T = (8, 128)
@@ -25,8 +25,8 @@
     res, ys, sums,
     mat, sup, weight, spring, diag, kf, kv, iw,
     vf, pe, co, sr, sl, sc, hl, hr, rc, pr, ring,
-    fsu, fsd, fu, fd, fl, fr, moments, tsum, pa, pb,
-    in_sem, dsend, drecv, fsend, frecv, psend, precv,
+    fsu, fsd, fu, fd, fl, fr, moments, tsum, row, slots,
+    spread, in_sem, dsend, drecv, fsend, frecv, psend, precv,
 ):
     na, nh = lax.axis_size("ang"), lax.axis_size("hgt")
     me_a, me_h = lax.axis_index("ang"), lax.axis_index("hgt")
@@ -64,19 +64,33 @@
 
     barrier = pltpu.get_barrier_semaphore()
 
-    def greet_a(d, carry):
-        pl.semaphore_signal(barrier, inc=1, device_id={"ang": lax.rem(me_a + d, na), "hgt": me_h}, device_id_type=MESH)
-        return carry
-
-    def greet_h(d, carry):
-        pl.semaphore_signal(barrier, inc=1, device_id={"ang": me_a, "hgt": lax.rem(me_h + d, nh)}, device_id_type=MESH)
-        return carry
-
-    for da, dh in SHIFT[4:]:
-        guarded(dh, lambda da=da, dh=dh: pl.semaphore_signal(
-            barrier, inc=1, device_id=device(da, dh), device_id_type=MESH))
-    lax.fori_loop(1, na, greet_a, 0)
-    lax.fori_loop(1, nh, greet_h, 0)
+    def neighbour(da, dh, sem):
+        pl.semaphore_signal(sem, inc=1, device_id=device(da, dh), device_id_type=MESH)
+
+    for da, dh in SHIFT:
+        guarded(dh, lambda da=da, dh=dh: neighbour(da, dh, barrier))
+
+    rounds = ([(0, 1 << i) for i in range((na // 2 - 1).bit_length())]
+              + [(1, 1 << i) for i in range((nh - 1).bit_length())])
+
+    def far(r, body):
+        axis, d = rounds[r]
+        if axis == 0:
+            body(d, 0)
+            body(-d, 0)
+        else:
+            pl.when(me_h + d < nh)(lambda: body(0, d))
+            pl.when(me_h - d >= 0)(lambda: body(0, -d))
+
+    def tell(r):
+        if r < len(rounds):
+            far(r, lambda da, dh: neighbour(da, dh, spread.at[r]))
+
+    def hear(r):
+        if r < len(rounds):
+            axis, d = rounds[r]
+            many = 2 if axis == 0 else (me_h + d < nh).astype(jnp.int32) + (me_h - d >= 0).astype(jnp.int32)
+            pl.semaphore_wait(spread.at[r], many)
 
     def roll(x, shift, axis=0):
         return pltpu.roll(x, shift % x.shape[axis], axis)
@@ -138,7 +152,7 @@
             device_id=device(*SHIFT[d]), device_id_type=MESH)
 
     def deep_start(k, slot, first, count):
-        for d in (UP, DOWN, RU, LU, RD, LD, RIGHT, LEFT):
+        for d in (RU, LU, RD, LD, RIGHT, LEFT, UP, DOWN):
             guarded(SHIFT[d][1], lambda d=d: deep(k, slot, first, count, d).start())
 
     def deep_wait(k, slot, first, count):
@@ -161,7 +175,7 @@
             device_id=device(*SHIFT[d]), device_id_type=MESH)
 
     def fine_start(k, g):
-        for d in range(4):
+        for d in (RIGHT, LEFT, UP, DOWN):
             guarded(SHIFT[d][1], lambda d=d: fine(k, g, d).start())
 
     def fine_wait(k, g):
@@ -243,8 +257,9 @@
     for d in (RU, LU, RD, LD):
         sc[d - 4, pcol // 2] = merge(d, tiles[d - 4], zero)
 
-    diagonals = 2 * (has_up.astype(jnp.int32) + has_down.astype(jnp.int32))
-    pl.semaphore_wait(barrier, na - 1 + nh - 1 + diagonals)
+    sides = has_up.astype(jnp.int32) + has_down.astype(jnp.int32)
+    pl.semaphore_wait(barrier, 2 + 3 * sides)
+    tell(0)
     deep_start(0, groups, pcol, 1)
 
     def restrict(k, c):
@@ -372,28 +387,41 @@
             rows = zero
             for m in range(2 * STEPS):
                 rows = jnp.where(sub == m, jnp.sum(moments[c, m], axis=0, keepdims=True), rows)
-            tsum[0] += jnp.where(lane == c, jnp.sum(rows, axis=1, keepdims=True), 0.0)
-
-    def psum(stage):
-        n, me, slots = (na, me_a, pa) if stage == 0 else (nh, me_h, pb)
-
-        def one(d, carry):
-            other = lax.rem(me + d, n)
-            where = {"ang": other, "hgt": me_h} if stage == 0 else {"ang": me_a, "hgt": other}
+            tsum[...] += jnp.where(lane == sub * cols + c, jnp.sum(rows, axis=1, keepdims=True), 0.0)
+
+    def total_moments():
+        n, me = na * nh, me_a * nh + me_h
+        row[0] = jnp.sum(tsum[...], axis=0, keepdims=True)
+
+        core, x, z_hi = lax.rem(me_a, 2), lax.rem(me_a // 2, na // 4), me_a // (na // 2)
+        y, z = lax.rem(me_h, nh // 2), 2 * z_hi + me_h // (nh // 2)
+        nx, ny = na // 4, nh // 2
+
+        def order(q):
+            return jnp.where(q == 0, 2, jnp.where(q == 1, 1, jnp.where(q == 2, 3, 0)))
+
+        def one(i, carry):
+            to_core = lax.rem(core + 1 - lax.rem(i, 2), 2)
+            to_x = lax.rem(x + order(lax.rem(i // 2, nx)), nx)
+            to_y = lax.rem(y + order(lax.rem(i // (2 * nx), ny)), ny)
+            to_z = lax.rem(z + order(i // (2 * nx * ny)), 4)
+            to = {"ang": (to_z // 2 * nx + to_x) * 2 + to_core, "hgt": lax.rem(to_z, 2) * ny + to_y}
             pltpu.make_async_remote_copy(
-                src_ref=tsum.at[stage], dst_ref=slots.at[me], send_sem=psend.at[stage], recv_sem=precv.at[stage],
-                device_id=where, device_id_type=MESH).start()
-            return carry
-
-        lax.fori_loop(1, n, one, 0)
-        slots[me] = tsum[stage]
+                src_ref=row.at[0], dst_ref=slots.at[me], send_sem=psend, recv_sem=precv,
+                device_id=to, device_id_type=MESH).start()
+            return carry
+
+        lax.fori_loop(0, n - 1, one, 0)
+        slots[me] = row[0]
         many = slots.at[pl.ds(0, n - 1)]
-        pltpu.make_async_copy(many, many, psend.at[stage]).wait()
-        pltpu.make_async_copy(many, many, precv.at[stage]).wait()
-        total = slots[0]
-        for i in range(1, n):
-            total = total + slots[i]
-        return total
+        pltpu.make_async_copy(many, many, psend).wait()
+        pltpu.make_async_copy(many, many, precv).wait()
+        parts = [slots[i] for i in range(8)]
+        for i in range(8, n):
+            parts[i % 8] = parts[i % 8] + slots[i]
+        while len(parts) > 1:
+            parts = [x + y for x, y in zip(parts[::2], parts[1::2])]
+        return parts[0]
 
     def stage(s, g):
         if s == 0:
@@ -405,30 +433,30 @@
             if s == 2 * STEPS:
                 reduce_moments(g)
 
-    tsum[0] = zero
-    for t in range(2 * STEPS + 2):
+    tsum[...] = zero
+    for t in range(2 * STEPS + 1):
         if t == 1:
             pl.when(jnp.logical_not(has_down))(lambda: clear(0, (RU - 4, LU - 4), fd))
             pl.when(jnp.logical_not(has_up))(lambda: clear(7, (RD - 4, LD - 4), fu))
             coarse_ring()
-
-        def both(i, carry):
-            if t <= 2 * STEPS:
-                stage(t, 2 * i)
-            if t >= 1:
-                stage(t - 1, 2 * i + 1)
-            return carry
-
-        lax.fori_loop(0, groups // 2, both, 0)
-
-    tsum[1] = psum(0)
-    sums[...] = psum(1)
-
-
-def combine(sums, res, ys, out_x, out_r):
-    m = [sums[i:i + 1, :] for i in range(2 * STEPS)]
-    none = jnp.zeros_like(m[0])
-    one = jnp.ones_like(m[0])
+        lax.fori_loop(0, groups, lambda g, carry: (stage(t, g), carry)[1], 0)
+        for r in range(2 * t - 2, 2 * t):
+            if r >= 0:
+                hear(r)
+                tell(r + 1)
+
+    sums[...] = total_moments()
+
+
+def combine(sums, res, ys, out_x, out_r, coef, xs, rs, sem):
+    cols, flat, _ = out_x.shape
+    shape = (16, 128)
+    sub = lax.broadcasted_iota(jnp.int32, shape, 0)
+    lane = lax.broadcasted_iota(jnp.int32, shape, 1)
+    m = [jnp.broadcast_to(jnp.sum(jnp.where(lane == sub + i * cols, sums[...], 0.0), axis=1, keepdims=True), shape)
+         for i in range(2 * STEPS)]
+    none = jnp.zeros(shape, F32)
+    one = jnp.ones(shape, F32)
     way, left, made = [one, none, none], [one, none, none, none], [none] * 3
     rz = m[0]
     for k in range(STEPS):
@@ -451,20 +479,29 @@
             beta = new / rz
             way = [left[j] + beta * way[j] for j in range(3)]
             rz = new
-
-    c = pl.program_id(0)
-    lane = lax.broadcasted_iota(jnp.int32, (1, 128), 1)
-
-    def pick(x):
-        return jnp.broadcast_to(jnp.sum(jnp.where(lane == c, x, 0.0), axis=1, keepdims=True), T)
-
-    x_of = [pick(x) for x in made]
-    r_of = [pick(x) for x in left]
-    for a in range(out_x.shape[1] // 8):
-        rows = pl.ds(8 * a, 8)
-        out_x[0, rows, :] = x_of[0] * ys[0, c, rows, :] + x_of[1] * ys[1, c, rows, :] + x_of[2] * ys[2, c, rows, :]
-        out_r[0, rows, :] = (r_of[0] * res[0, c, rows, :] + r_of[1] * res[1, c, rows, :]
-                             + r_of[2] * res[2, c, rows, :] + r_of[3] * res[3, c, rows, :])
+    for i, x in enumerate(made + left):
+        coef[i] = x
+
+    def copies(c):
+        return (pltpu.make_async_copy(xs.at[c], out_x.at[c], sem.at[0, c]),
+                pltpu.make_async_copy(rs.at[c], out_r.at[c], sem.at[1, c]))
+
+    def column(c, carry):
+        x_of = [jnp.broadcast_to(coef[i, pl.ds(c, 1), :], T) for i in range(3)]
+        r_of = [jnp.broadcast_to(coef[3 + i, pl.ds(c, 1), :], T) for i in range(4)]
+        for a in range(flat // 8):
+            rows = pl.ds(8 * a, 8)
+            xs[c, rows, :] = x_of[0] * ys[0, c, rows, :] + x_of[1] * ys[1, c, rows, :] + x_of[2] * ys[2, c, rows, :]
+            rs[c, rows, :] = (r_of[0] * res[0, c, rows, :] + r_of[1] * res[1, c, rows, :]
+                              + r_of[2] * res[2, c, rows, :] + r_of[3] * res[3, c, rows, :])
+        for copy in copies(c):
+            copy.start()
+        return carry
+
+    lax.fori_loop(0, cols, column, 0)
+    for c in range(cols):
+        for copy in copies(c):
+            copy.wait()
 
 
 def body(loads, material, support, modulus, positions):
@@ -472,15 +509,15 @@
     cols = cases * comps
     na, nh = lax.axis_size("ang"), lax.axis_size("hgt")
     flat = angs * rows
-    any_spec = pl.BlockSpec(memory_space=pltpu.HBM)
+    hbm = pl.BlockSpec(memory_space=pltpu.HBM)
     smem = pl.BlockSpec(memory_space=pltpu.SMEM)
     vmem = pl.BlockSpec(memory_space=pltpu.VMEM)
     v = lambda *shape: pltpu.VMEM((*shape, 128), F32)
     dma = lambda *shape: pltpu.SemaphoreType.DMA(shape)
     res, ys, sums = pl.pallas_call(
         kernel,
-        out_shape=(v(STEPS + 1, cols, flat), v(STEPS, cols, flat), v(8)),
-        in_specs=[smem, smem, any_spec, any_spec, any_spec],
+        out_shape=(v(STEPS + 1, cols, flat), v(STEPS, cols, flat), v(1)),
+        in_specs=[smem, smem, hbm, hbm, hbm],
         out_specs=(vmem, vmem, vmem),
         scratch_shapes=[
             pltpu.VMEM((flat, 128), jnp.int32), pltpu.VMEM((flat, 128), jnp.int32),
@@ -492,22 +529,21 @@
             v(8, 3, 8), v(3, 2, 8, 3, 8),
             v(cols, 32), v(cols, 32), v(STEPS, cols, 32), v(STEPS, cols, 32),
             v(STEPS, cols, 8), v(STEPS, cols, 8),
-            v(cols, 2 * STEPS, 8), v(2, 8), v(na, 8), v(nh, 8),
-            dma(GROUPS + 2), dma(STEPS, GROUPS + 1, 8), dma(STEPS, GROUPS + 1, 8),
-            dma(STEPS, GROUPS, 4), dma(STEPS, GROUPS, 4), dma(2), dma(2),
+            v(cols, 2 * STEPS, 8), v(8), v(1, 1), v(na * nh, 1),
+            pltpu.SemaphoreType.REGULAR((8,)), dma(GROUPS + 2), dma(STEPS, GROUPS + 1, 8), dma(STEPS, GROUPS + 1, 8),
+            dma(STEPS, GROUPS, 4), dma(STEPS, GROUPS, 4), pltpu.SemaphoreType.DMA, pltpu.SemaphoreType.DMA,
         ],
         compiler_params=pltpu.CompilerParams(
             collective_id=0, has_side_effects=True, vmem_limit_bytes=55 * 1000 * 1000),
         name="girder_cg",
     )(modulus, positions, loads.reshape(cols, flat, radial), material.reshape(flat, radial), support.reshape(flat, radial))
     out = jax.ShapeDtypeStruct((cols, flat, radial), F32)
-    block = pl.BlockSpec((1, flat, radial), lambda c: (c, 0, 0))
     x, r = pl.pallas_call(
         combine,
-        grid=(cols,),
         out_shape=(out, out),
         in_specs=[vmem, vmem, vmem],
-        out_specs=(block, block),
+        out_specs=(hbm, hbm),
+        scratch_shapes=[v(2 * STEPS + 1, 16), v(cols, flat), v(cols, flat), dma(2, cols)],
         compiler_params=pltpu.CompilerParams(vmem_limit_bytes=16 * 1024 * 1024),
         name="girder_combine",
     )(sums, res, ys)

time: 73.9 us -> 69 us (0.934)
  Pallas kernels: 73.1 us -> 68.2 us
    pallas_call x1, Pallas kernels: 5.46 us -> 2.03 us  [body(): pl.pallas_call(combine, out_shape=(out, out), in_specs=[vmem, vmem, vmem]...]
    pallas_call x1, Pallas kernels: 67.6 us -> 66.2 us  [body(): pl.pallas_call(kernel, out_shape=(v(STEPS + 1, cols, flat), v(STEPS, cols...]
where the time goes in v3:
time: 69 us; the launch traced here: 68.9 us
  Pallas kernels  68.2 us (99%)
    pallas_call x1, Pallas kernels, body(): pl.pallas_call(kernel, out_shape=(v(STEPS + 1, cols, flat), v(STEPS, cols...  66.2 us
    pallas_call x1, Pallas kernels, body(): pl.pallas_call(combine, out_shape=(out, out), in_specs=[vmem, vmem, vmem]...  2.03 us

profile of v3, /device:TPU:1, one launch (start us, length us, event | category | flops | bytes accessed | tf_op | source)
XLA Modules:
  0.0 68.9 jit_solution(7238607488399048477)
XLA Ops:
  0.6 66.2 %girder_cg.1 = (f32[4,12,256,128]{3,2,1,0:T(8,128)S(1)}, f32[3,12,256,128]{3,2,1,0:T(8,128)S(1)}, f32[1,128]{1,0:T(1,128)S(1)}) custom-call(f32[8]{0:T(128)} %modulus.1, s32[4]{0:T(128)} %positions.1, f32[12,256,128]{2,1,0:T(8,128)} %bitcast.5, s32[256,128]{1,0:T(8,128)} %bitcast.6, s32[256,128]{1,0:T(8,128)} %bitcast.7), custom_call_target="tpu_custom_call" | custom-call | tf_op jit(solution)/shard_map/girder_cg/pallas_call | solution.py:517
  66.8 2.0 %girder_combine.1 = (f32[12,256,128]{2,1,0:T(8,128)}, f32[12,256,128]{2,1,0:T(8,128)}) custom-call(f32[1,128]{1,0:T(1,128)S(1)} %get-tuple-element.7.sums, f32[4,12,256,128]{3,2,1,0:T(8,128)S(1)} %get-tuple-element.8.res, f32[3,12,256,128]{3,2,1,0:T(8,128)S(1)} %get-tuple-element.9.ys), custom_call_target="tpu_custom_call" | custom-call | tf_op jit(solution)/shard_map/girder_combine/pallas_call | solution.py:541

commit v4 on v3

--- a/solution.py
+++ b/solution.py
@@ -393,25 +393,14 @@
         n, me = na * nh, me_a * nh + me_h
         row[0] = jnp.sum(tsum[...], axis=0, keepdims=True)
 
-        core, x, z_hi = lax.rem(me_a, 2), lax.rem(me_a // 2, na // 4), me_a // (na // 2)
-        y, z = lax.rem(me_h, nh // 2), 2 * z_hi + me_h // (nh // 2)
-        nx, ny = na // 4, nh // 2
-
-        def order(q):
-            return jnp.where(q == 0, 2, jnp.where(q == 1, 1, jnp.where(q == 2, 3, 0)))
-
-        def one(i, carry):
-            to_core = lax.rem(core + 1 - lax.rem(i, 2), 2)
-            to_x = lax.rem(x + order(lax.rem(i // 2, nx)), nx)
-            to_y = lax.rem(y + order(lax.rem(i // (2 * nx), ny)), ny)
-            to_z = lax.rem(z + order(i // (2 * nx * ny)), 4)
-            to = {"ang": (to_z // 2 * nx + to_x) * 2 + to_core, "hgt": lax.rem(to_z, 2) * ny + to_y}
+        def one(d, carry):
+            other = lax.rem(me + d, n)
             pltpu.make_async_remote_copy(
                 src_ref=row.at[0], dst_ref=slots.at[me], send_sem=psend, recv_sem=precv,
-                device_id=to, device_id_type=MESH).start()
-            return carry
-
-        lax.fori_loop(0, n - 1, one, 0)
+                device_id={"ang": other // nh, "hgt": lax.rem(other, nh)}, device_id_type=MESH).start()
+            return carry
+
+        lax.fori_loop(1, n, one, 0)
         slots[me] = row[0]
         many = slots.at[pl.ds(0, n - 1)]
         pltpu.make_async_copy(many, many, psend).wait()
@@ -440,10 +429,9 @@
             pl.when(jnp.logical_not(has_up))(lambda: clear(7, (RD - 4, LD - 4), fu))
             coarse_ring()
         lax.fori_loop(0, groups, lambda g, carry: (stage(t, g), carry)[1], 0)
-        for r in range(2 * t - 2, 2 * t):
-            if r >= 0:
-                hear(r)
-                tell(r + 1)
+        if t >= 1:
+            hear(t - 1)
+            tell(t)
 
     sums[...] = total_moments()
 

time: 69 us -> 65.4 us (0.948)
  Pallas kernels: 68.2 us -> 64.6 us
    pallas_call x1, Pallas kernels: 66.2 us -> 62.5 us  [body(): pl.pallas_call(kernel, out_shape=(v(STEPS + 1, cols, flat), v(STEPS, cols...]
where the time goes in v4:
time: 65.4 us; the launch traced here: 65.2 us
  Pallas kernels  64.6 us (99%)
    pallas_call x1, Pallas kernels, body(): pl.pallas_call(kernel, out_shape=(v(STEPS + 1, cols, flat), v(STEPS, cols...  62.5 us
    pallas_call x1, Pallas kernels, body(): pl.pallas_call(combine, out_shape=(out, out), in_specs=[vmem, vmem, vmem]...  2.03 us

profile of v4, /device:TPU:1, one launch (start us, length us, event | category | flops | bytes accessed | tf_op | source)
XLA Modules:
  0.0 65.2 jit_solution(16114756495112917479)
XLA Ops:
  0.6 62.5 %girder_cg.1 = (f32[4,12,256,128]{3,2,1,0:T(8,128)S(1)}, f32[3,12,256,128]{3,2,1,0:T(8,128)S(1)}, f32[1,128]{1,0:T(1,128)S(1)}) custom-call(f32[8]{0:T(128)} %modulus.1, s32[4]{0:T(128)} %positions.1, f32[12,256,128]{2,1,0:T(8,128)} %bitcast.5, s32[256,128]{1,0:T(8,128)} %bitcast.6, s32[256,128]{1,0:T(8,128)} %bitcast.7), custom_call_target="tpu_custom_call" | custom-call | tf_op jit(solution)/shard_map/girder_cg/pallas_call | solution.py:505
  63.2 2.0 %girder_combine.1 = (f32[12,256,128]{2,1,0:T(8,128)}, f32[12,256,128]{2,1,0:T(8,128)}) custom-call(f32[1,128]{1,0:T(1,128)S(1)} %get-tuple-element.7.sums, f32[4,12,256,128]{3,2,1,0:T(8,128)S(1)} %get-tuple-element.8.res, f32[3,12,256,128]{3,2,1,0:T(8,128)S(1)} %get-tuple-element.9.ys), custom_call_target="tpu_custom_call" | custom-call | tf_op jit(solution)/shard_map/girder_combine/pallas_call | solution.py:529

commit v5 on v4

--- a/solution.py
+++ b/solution.py
@@ -160,28 +160,43 @@
             guarded(SHIFT[d][1], lambda d=d: deep(k, slot, first, count, d).wait_send())
             guarded(-SHIFT[d][1], lambda d=d: deep(k, slot, first, count, d).wait_recv())
 
-    def fine(k, g, d):
+    half = angs // 2
+
+    def fine_parts(d, part):
+        if part is None:
+            return pl.ds(0, angs)
+        if d == UP:
+            return pl.ds(half, half) if part == 0 else pl.ds(0, half)
+        if d == DOWN:
+            return pl.ds(0, half) if part == 0 else pl.ds(half, half)
+        return None if (d == LEFT) != (part == 0) else pl.ds(0, angs)
+
+    def fine(k, g, d, part):
         c = pl.ds(g * per, per)
+        rows = fine_parts(d, part)
         if d == UP:
-            src, dst = fsu.at[c], fd.at[k, c]
+            src, dst = fsu.at[c, rows], fd.at[k, c, rows]
         elif d == DOWN:
-            src, dst = fsd.at[c], fu.at[k, c]
+            src, dst = fsd.at[c, rows], fu.at[k, c, rows]
         elif d == RIGHT:
             src, dst = vf.at[c, pl.ds(8 * (angs - 1), 8)], fl.at[k, c]
         else:
             src, dst = vf.at[c, pl.ds(0, 8)], fr.at[k, c]
+        i = d + 4 if part == 1 else d
         return pltpu.make_async_remote_copy(
-            src_ref=src, dst_ref=dst, send_sem=fsend.at[k, g, d], recv_sem=frecv.at[k, g, d],
+            src_ref=src, dst_ref=dst, send_sem=fsend.at[k, g, i], recv_sem=frecv.at[k, g, i],
             device_id=device(*SHIFT[d]), device_id_type=MESH)
 
-    def fine_start(k, g):
+    def fine_start(k, g, part):
         for d in (RIGHT, LEFT, UP, DOWN):
-            guarded(SHIFT[d][1], lambda d=d: fine(k, g, d).start())
-
-    def fine_wait(k, g):
+            if fine_parts(d, part) is not None:
+                guarded(SHIFT[d][1], lambda d=d: fine(k, g, d, part).start())
+
+    def fine_wait(k, g, part):
         for d in range(4):
-            guarded(SHIFT[d][1], lambda d=d: fine(k, g, d).wait_send())
-            guarded(-SHIFT[d][1], lambda d=d: fine(k, g, d).wait_recv())
+            if fine_parts(d, part) is not None:
+                guarded(SHIFT[d][1], lambda d=d: fine(k, g, d, part).wait_send())
+                guarded(-SHIFT[d][1], lambda d=d: fine(k, g, d, part).wait_recv())
 
     def corner_tiles(k, c):
         low = [co[k, c, 3 + h, pl.ds(0, 8), :] for h in range(4)]
@@ -327,15 +342,24 @@
                                 pe[parity, pl.ds(b * 128 + da * 8 + 2 * h + dh, 8, stride=16), :] = new
 
     def prolong(k, g, c, parity):
-        acc = zero
+        last = k == STEPS - 1
+        acc, square, edges, before = zero, zero, zero, None
         for a in range(angs):
             rows = pl.ds(8 * a, 8)
             r = res[k, c, rows, :]
             z = kf[rows, :] * r + pe[parity, rows, :]
             ys[k, c, rows, :] = z
             acc = acc + r * z
-            vf[c, rows, :] = weight[rows, :] * z
+            v = weight[rows, :] * z
+            vf[c, rows, :] = v
+            if last:
+                ahead = jnp.where(sub == 7, 0.0, roll(v, -1)) + jnp.where(lane == 127, 0.0, roll(v, -1, 1))
+                square = square + diag[rows, :] * z * z
+                edges = edges + v * (ahead if a == 0 else ahead + before)
+                before = v
         moments[c, 2 * k] = acc
+        if last:
+            moments[c, 2 * k + 1] = square - 2.0 * edges - acc
         for i in range(4):
             fsu[c, pl.ds(8 * i, 8), :] = vf[c, pl.ds(64 * i + 7, 8, stride=8), :]
             fsd[c, pl.ds(8 * i, 8), :] = vf[c, pl.ds(64 * i, 8, stride=8), :]
@@ -352,10 +376,10 @@
             return carry
 
         lax.fori_loop(0, per // 2, pair_body, 0)
-        fine_start(k, g)
+        fine_start(k, g, None if k < STEPS - 1 else 0)
 
     def apply_fine(k, g):
-        fine_wait(k, g)
+        fine_wait(k, g, None if k < STEPS - 1 else 1)
 
         def column(i, carry):
             c = g * per + i
@@ -372,8 +396,8 @@
                 res[k + 1, c, rows, :] = r
                 acc = acc + r * z
                 before, now = now, after
-            moments[c, 2 * k + 1] = acc
             if k + 1 < STEPS:
+                moments[c, 2 * k + 1] = acc
                 restrict(k + 1, c)
             return carry
 
@@ -402,6 +426,7 @@
 
         lax.fori_loop(1, n, one, 0)
         slots[me] = row[0]
+        lax.fori_loop(0, groups, lambda g, carry: (apply_fine(STEPS - 1, g), carry)[1], 0)
         many = slots.at[pl.ds(0, n - 1)]
         pltpu.make_async_copy(many, many, psend).wait()
         pltpu.make_async_copy(many, many, precv).wait()
@@ -412,15 +437,27 @@
             parts = [x + y for x, y in zip(parts[::2], parts[1::2])]
         return parts[0]
 
+    def outer_edges(g):
+        k = STEPS - 1
+        fine_wait(k, g, 0)
+        for i in range(per):
+            c = g * per + i
+            edges = vf[c, pl.ds(8 * (angs - 1), 8), :] * fr[k, c]
+            for at in range(0, half, 8):
+                low, high = pl.ds(at, 8), pl.ds(half + at, 8)
+                edges = edges + fsu[c, low, :] * fu[k, c, low, :] + fsd[c, high, :] * fd[k, c, high, :]
+            moments[c, 2 * k + 1] = moments[c, 2 * k + 1] - 2.0 * edges
+
     def stage(s, g):
         if s == 0:
             first(g)
         elif s % 2:
             precondition(s // 2, g)
+        elif s < 2 * STEPS:
+            apply_fine(s // 2 - 1, g)
         else:
-            apply_fine(s // 2 - 1, g)
-            if s == 2 * STEPS:
-                reduce_moments(g)
+            outer_edges(g)
+            reduce_moments(g)
 
     tsum[...] = zero
     for t in range(2 * STEPS + 1):
@@ -432,6 +469,8 @@
         if t >= 1:
             hear(t - 1)
             tell(t)
+        if t == 2 * STEPS - 1:
+            lax.fori_loop(0, groups, lambda g, carry: (fine_start(STEPS - 1, g, 1), carry)[1], 0)
 
     sums[...] = total_moments()
 
@@ -519,7 +558,7 @@
             v(STEPS, cols, 8), v(STEPS, cols, 8),
             v(cols, 2 * STEPS, 8), v(8), v(1, 1), v(na * nh, 1),
             pltpu.SemaphoreType.REGULAR((8,)), dma(GROUPS + 2), dma(STEPS, GROUPS + 1, 8), dma(STEPS, GROUPS + 1, 8),
-            dma(STEPS, GROUPS, 4), dma(STEPS, GROUPS, 4), pltpu.SemaphoreType.DMA, pltpu.SemaphoreType.DMA,
+            dma(STEPS, GROUPS, 8), dma(STEPS, GROUPS, 8), pltpu.SemaphoreType.DMA, pltpu.SemaphoreType.DMA,
         ],
         compiler_params=pltpu.CompilerParams(
             collective_id=0, has_side_effects=True, vmem_limit_bytes=55 * 1000 * 1000),

time: 65.4 us -> 64.7 us (0.989)
  Pallas kernels: 64.6 us -> 63.9 us
    pallas_call x1, Pallas kernels: 62.5 us -> 61.9 us  [body(): pl.pallas_call(kernel, out_shape=(v(STEPS + 1, cols, flat), v(STEPS, cols...]
where the time goes in v5:
time: 64.7 us; the launch traced here: 64.5 us
  Pallas kernels  63.9 us (99%)
    pallas_call x1, Pallas kernels, body(): pl.pallas_call(kernel, out_shape=(v(STEPS + 1, cols, flat), v(STEPS, cols...  61.9 us
    pallas_call x1, Pallas kernels, body(): pl.pallas_call(combine, out_shape=(out, out), in_specs=[vmem, vmem, vmem]...  2.03 us

profile of v5, /device:TPU:1, one launch (start us, length us, event | category | flops | bytes accessed | tf_op | source)
XLA Modules:
  0.0 64.5 jit_solution(10514145959236104468)
XLA Ops:
  0.6 61.9 %girder_cg.1 = (f32[4,12,256,128]{3,2,1,0:T(8,128)S(1)}, f32[3,12,256,128]{3,2,1,0:T(8,128)S(1)}, f32[1,128]{1,0:T(1,128)S(1)}) custom-call(f32[8]{0:T(128)} %modulus.1, s32[4]{0:T(128)} %positions.1, f32[12,256,128]{2,1,0:T(8,128)} %bitcast.5, s32[256,128]{1,0:T(8,128)} %bitcast.6, s32[256,128]{1,0:T(8,128)} %bitcast.7), custom_call_target="tpu_custom_call" | custom-call | tf_op jit(solution)/shard_map/girder_cg/pallas_call | solution.py:544
  62.5 2.0 %girder_combine.1 = (f32[12,256,128]{2,1,0:T(8,128)}, f32[12,256,128]{2,1,0:T(8,128)}) custom-call(f32[1,128]{1,0:T(1,128)S(1)} %get-tuple-element.7.sums, f32[4,12,256,128]{3,2,1,0:T(8,128)S(1)} %get-tuple-element.8.res, f32[3,12,256,128]{3,2,1,0:T(8,128)S(1)} %get-tuple-element.9.ys), custom_call_target="tpu_custom_call" | custom-call | tf_op jit(solution)/shard_map/girder_combine/pallas_call | solution.py:568

commit v6 on v5

--- a/solution.py
+++ b/solution.py
@@ -424,7 +424,7 @@
                 device_id={"ang": other // nh, "hgt": lax.rem(other, nh)}, device_id_type=MESH).start()
             return carry
 
-        lax.fori_loop(1, n, one, 0)
+        lax.fori_loop(1, n, one, 0, unroll=True)
         slots[me] = row[0]
         lax.fori_loop(0, groups, lambda g, carry: (apply_fine(STEPS - 1, g), carry)[1], 0)
         many = slots.at[pl.ds(0, n - 1)]

time: 64.7 us -> 64.5 us (level)
  no operation moved by 1% of the time
where the time goes in v6:
time: 64.5 us; the launch traced here: 64.4 us
  Pallas kernels  63.7 us (99%)
    pallas_call x1, Pallas kernels, body(): pl.pallas_call(kernel, out_shape=(v(STEPS + 1, cols, flat), v(STEPS, cols...  61.7 us
    pallas_call x1, Pallas kernels, body(): pl.pallas_call(combine, out_shape=(out, out), in_specs=[vmem, vmem, vmem]...  2.03 us

profile of v6, /device:TPU:1, one launch (start us, length us, event | category | flops | bytes accessed | tf_op | source)
XLA Modules:
  0.0 64.4 jit_solution(14147169269726465873)
XLA Ops:
  0.6 61.7 %girder_cg.1 = (f32[4,12,256,128]{3,2,1,0:T(8,128)S(1)}, f32[3,12,256,128]{3,2,1,0:T(8,128)S(1)}, f32[1,128]{1,0:T(1,128)S(1)}) custom-call(f32[8]{0:T(128)} %modulus.1, s32[4]{0:T(128)} %positions.1, f32[12,256,128]{2,1,0:T(8,128)} %bitcast.5, s32[256,128]{1,0:T(8,128)} %bitcast.6, s32[256,128]{1,0:T(8,128)} %bitcast.7), custom_call_target="tpu_custom_call" | custom-call | tf_op jit(solution)/shard_map/girder_cg/pallas_call | solution.py:544
  62.3 2.0 %girder_combine.1 = (f32[12,256,128]{2,1,0:T(8,128)}, f32[12,256,128]{2,1,0:T(8,128)}) custom-call(f32[1,128]{1,0:T(1,128)S(1)} %get-tuple-element.7.sums, f32[4,12,256,128]{3,2,1,0:T(8,128)S(1)} %get-tuple-element.8.res, f32[3,12,256,128]{3,2,1,0:T(8,128)S(1)} %get-tuple-element.9.ys), custom_call_target="tpu_custom_call" | custom-call | tf_op jit(solution)/shard_map/girder_combine/pallas_call | solution.py:568

commit v7 on v6

--- a/solution.py
+++ b/solution.py
@@ -152,7 +152,7 @@
             device_id=device(*SHIFT[d]), device_id_type=MESH)
 
     def deep_start(k, slot, first, count):
-        for d in (RU, LU, RD, LD, RIGHT, LEFT, UP, DOWN):
+        for d in (UP, DOWN, RIGHT, LEFT, RU, LU, RD, LD):
             guarded(SHIFT[d][1], lambda d=d: deep(k, slot, first, count, d).start())
 
     def deep_wait(k, slot, first, count):

time: 64.5 us -> 64.9 us (level)
  no operation moved by 1% of the time
where the time goes in v7:
time: 64.9 us; the launch traced here: 64.8 us
  Pallas kernels  64.1 us (99%)
    pallas_call x1, Pallas kernels, body(): pl.pallas_call(kernel, out_shape=(v(STEPS + 1, cols, flat), v(STEPS, cols...  62.1 us
    pallas_call x1, Pallas kernels, body(): pl.pallas_call(combine, out_shape=(out, out), in_specs=[vmem, vmem, vmem]...  2.03 us

profile of v7, /device:TPU:1, one launch (start us, length us, event | category | flops | bytes accessed | tf_op | source)
XLA Modules:
  0.0 64.8 jit_solution(4544728562714764769)
XLA Ops:
  0.6 62.1 %girder_cg.1 = (f32[4,12,256,128]{3,2,1,0:T(8,128)S(1)}, f32[3,12,256,128]{3,2,1,0:T(8,128)S(1)}, f32[1,128]{1,0:T(1,128)S(1)}) custom-call(f32[8]{0:T(128)} %modulus.1, s32[4]{0:T(128)} %positions.1, f32[12,256,128]{2,1,0:T(8,128)} %bitcast.5, s32[256,128]{1,0:T(8,128)} %bitcast.6, s32[256,128]{1,0:T(8,128)} %bitcast.7), custom_call_target="tpu_custom_call" | custom-call | tf_op jit(solution)/shard_map/girder_cg/pallas_call | solution.py:544
  62.8 2.0 %girder_combine.1 = (f32[12,256,128]{2,1,0:T(8,128)}, f32[12,256,128]{2,1,0:T(8,128)}) custom-call(f32[1,128]{1,0:T(1,128)S(1)} %get-tuple-element.7.sums, f32[4,12,256,128]{3,2,1,0:T(8,128)S(1)} %get-tuple-element.8.res, f32[3,12,256,128]{3,2,1,0:T(8,128)S(1)} %get-tuple-element.9.ys), custom_call_target="tpu_custom_call" | custom-call | tf_op jit(solution)/shard_map/girder_combine/pallas_call | solution.py:568
